TPU v7x, 256 devices: a whole 4x4x8 slice. The times are simulated.
256 devices in a mesh: row: 16 (over y, z_lo, core), col: 16 (over x, z_hi).
Axes of the slice: x: 4, y: 4, z: 8 (z_hi: 4, z_lo: 2; z = z_hi * 2 + z_lo), core: 2. Of those that a mesh axis runs over, the one named last changes fastest.
Arguments:
- fisher: float32 [16384, 16384], P('row', 'col'), may hold values from -6 to 6
- slab: float32 [2048, 16384], P(('row', 'col')), may hold values from -6 to 6
Outputs:
- fisher_out: float32 [16384, 16384], P('row', 'col')
All inputs are finite; a program needn't handle non-finite values.
Results may differ from a plain program's by a relative error of at most 0.00005.
Values sent between devices are 32-bit elements; how exact they have to be, the bound alone decides.
No kernel may reach another device: no remote copies, remote signals or barrier semaphores. Data moves between devices by JAX's collectives and lax.ppermute only.
A program may use at most 128 MiB of HBM per device.

v0:
```python
import jax
import jax.numpy as jnp
from jax import lax
from jax.sharding import PartitionSpec as P


def transposed_product(left, right):
    return lax.dot_general(
        left,
        right,
        (((0, 1, 2), (0, 1, 2)), ((), ())),
        precision=lax.Precision.HIGHEST,
        preferred_element_type=jnp.float32,
    )


def row_panel(slab, n_row, t_row):
    rows = slab.shape[0]
    pieces = lax.all_to_all(
        slab.reshape(rows, n_row, t_row), "row", split_axis=1, concat_axis=1, tiled=True
    )
    return lax.all_gather(pieces.reshape(rows, n_row, 1, t_row), "col", axis=2, tiled=True)


def col_pieces(slab, n_col, t_col):
    rows = slab.shape[0]
    pieces = lax.all_to_all(
        slab.reshape(rows, n_col, t_col), "col", split_axis=1, concat_axis=1, tiled=True
    )
    return pieces.reshape(rows, 1, n_col, t_col)


def direct_product(slab, n_row, n_col, t_row, t_col):
    left = row_panel(slab, n_row, t_row)
    local_right = col_pieces(slab, n_col, t_col)
    return transposed_product(left, lax.all_gather(local_right, "row", axis=1, tiled=True))


def body(fisher, slab):
    n_row = lax.axis_size("row")
    n_col = lax.axis_size("col")
    order = slab.shape[1]
    t_row = order // n_row
    t_col = order // n_col
    examples = slab.shape[0] * n_row * n_col
    product = direct_product(slab, n_row, n_col, t_row, t_col)
    return fisher + product / examples


def solution(mesh):
    return jax.shard_map(
        body,
        mesh=mesh,
        in_specs=(P("row", "col"), P(("row", "col"), None)),
        out_specs=P("row", "col"),
        check_vma=False,
    )
```

profile of v0, /device:TPU:37, one launch (start us, length us, event | category | flops | bytes accessed | tf_op | source)
XLA Modules:
  0.0 258.7 jit_solution(12735189172864952420)
XLA Ops:
  6.5 0.0 all-gather.7.cloned.1.call-start
  6.5 25.0 %all_to_all.10 = f32[8,16,1024]{2,0,1:T(8,128)} all-to-all(f32[8,16,1024]{2,0,1:T(8,128)} %bitcast.19), channel_id=1, replica_groups=mesh['row'=16,'col'=16] {'col'}, dimensions={1} | all-to-all | bytes 1048576 | tf_op jit(solution)/shard_map/all_to_all | solution.py:27
  31.5 0.0 all-gather.7.cloned.1.call-update
  31.6 0.0 all-gather.5.cloned.1.call-start
  31.6 19.5 %all_to_all.11 = f32[8,16,1024]{2,0,1:T(8,128)} all-to-all(f32[8,16,1024]{2,0,1:T(8,128)} %bitcast.20), channel_id=1, replica_groups=mesh['row'=16,'col'=16] {'row'}, dimensions={1} | all-to-all | bytes 1048576 | tf_op jit(solution)/shard_map/all_to_all | solution.py:19
  51.1 0.0 all-gather.5.cloned.1.call-update
  51.2 37.9 %all-gather.7.cloned.1.call-done = f32[8,256,1024]{2,0,1:T(8,128)} async-done(((f32[8,16,1024]{2,0,1:T(8,128)}), f32[8,256,1024]{2,0,1:T(8,128)}) %all-gather.7.cloned.1.call-update) | async-done | bytes 8388624 | tf_op jit(solution)/shard_map/all_gather | solution.py:36
  89.0 11.5 %copy.8 = f32[8,256,1024]{2,1,0:T(8,128)} copy(f32[8,256,1024]{2,0,1:T(8,128)} %all-gather.7.cloned.1.call-done) | data formatting | bytes 16777216 | tf_op jit(solution)/shard_map/all_gather | solution.py:36
  100.5 106.4 %all-gather.5.cloned.1.call-done = f32[8,16,16384]{2,0,1:T(8,128)} async-done(((f32[8,16,1024]{2,0,1:T(8,128)}), f32[8,16,16384]{2,0,1:T(8,128)}) %all-gather.5.cloned.1.call-update) | async-done | bytes 8388624 | tf_op jit(solution)/shard_map/all_gather | solution.py:22
  206.9 45.0 %fusion.2 = f32[1024,1024]{1,0:T(8,128)} fusion(f32[1024,1024]{1,0:T(8,128)} %param.2, f32[8,16,16,1024]{3,2,1,0:T(8,128)} %bitcast.18, f32[16,8,16,1024]{3,1,2,0:T(8,128)} %bitcast.21), kind=kOutput, calls=%fused_computation.4 | convolution fusion | flops 25771900928 | bytes 25165824 | tf_op jit(solution)/shard_map/dot_general | solution.py:8
Async XLA Ops:
  6.5 82.5 %all-gather.7.cloned.1.call-start = ((), (), s32[]{:S(2)}) async-start(), calls=%async_computation.3 | async-start | bytes 8912896 | tf_op jit(solution)/shard_map/all_gather | solution.py:36
  31.6 175.3 %all-gather.5.cloned.1.call-start = ((), (), s32[]{:S(2)}) async-start(), calls=%async_computation.2 | async-start | bytes 8912896 | tf_op jit(solution)/shard_map/all_gather | solution.py:22
Sparse Core Ops, SparseCore 0:
  31.7 57.3 all-gather.6
  91.5 115.2 all-gather.4
where the time goes:
time: 259 us
  waiting for transfers between devices  144 us (56%)
  matrix products  45 us (17%)
  blocking collectives  44.5 us (17%)
  between operations  13.4 us (5%)
  local copies, waits for them, and re-layouts  11.5 us (4%)
    all_gather x1, waiting for transfers between devices, row_panel(): lax.all_gather(pieces.reshape(rows, n_row, 1, t_row), 'col', axis=2, tile...  106 us
    dot_general x1, matrix products, transposed_product(): lax.dot_general(left, right, (((0, 1, 2), (0, 1, 2)), ((), ())), precisio...  45 us
    all_gather x1, waiting for transfers between devices, direct_product(): lax.all_gather(local_right, 'row', axis=1, tiled=True)  37.9 us
    all_to_all x1, blocking collectives, col_pieces(): lax.all_to_all(slab.reshape(rows, n_col, t_col), 'col', split_axis=1, con...  25 us
    all_to_all x1, blocking collectives, row_panel(): lax.all_to_all(slab.reshape(rows, n_row, t_row), 'row', split_axis=1, con...  19.5 us
    all_gather x1, local copies, waits for them, and re-layouts, direct_product(): lax.all_gather(local_right, 'row', axis=1, tiled=True)  11.5 us
  transfers between devices with their start and end apart: 2, of which 2 were waited for; matrix products, arithmetic and copies ran while one was open for 4% of the time, Pallas kernels for 0%

commit v1 on v0

v1 whole, which is shorter than its diff:
```python
import functools

import jax
import jax.numpy as jnp
from jax import lax
from jax.experimental import pallas as pl
from jax.experimental.pallas import tpu as pltpu
from jax.sharding import PartitionSpec as P


AXES = ("row", "col")
TILE_N = 512


def send(value, dy=0, dzl=0, dk=0, dx=0, dzh=0):
    pairs = []
    for y in range(4):
        for zl in range(2):
            for k in range(2):
                for x in range(4):
                    for zh in range(4):
                        here = (y * 4 + zl * 2 + k) * 16 + x * 4 + zh
                        there = (((y + dy) % 4) * 4 + (zl ^ dzl) * 2 + (k ^ dk)) * 16
                        there += ((x + dx) % 4) * 4 + (zh + dzh) % 4
                        pairs.append((there, here))
    return lax.ppermute(value, AXES, pairs)


def split(value):
    high = value.astype(jnp.bfloat16)
    return high, (value - high.astype(jnp.float32)).astype(jnp.bfloat16)


def kernel(row_classes, where_c, where_r, n_left, scale, place, acc, *refs):
    col_sets = len(where_r)
    left, right = refs[:n_left], refs[n_left : n_left + col_sets]
    r, c = place[0], place[1]
    from_row = [(((r >> 2) + dy) & 3) * 4 + (((r >> 1) & 1) ^ dzl) * 2 + ((r & 1) ^ dk) for dy, dzl, dk in where_r]
    from_col = [(((c >> 2) + dx) & 3) * 4 + (((c & 3) + dzh) & 3) for dx, dzh in where_c]
    out, lh, ll, rh, rl = refs[n_left + col_sets :]
    depth = 8 * col_sets

    @pl.when(pl.program_id(0) == 0)
    def _():
        for b, (which, base) in enumerate(row_classes):
            for pair in range(col_sets // 2):
                two = jnp.concatenate([left[which][base + from_row[2 * pair]], left[which][base + from_row[2 * pair + 1]]], axis=0)
                rows = pl.ds(b * depth + pair * 16, 16)
                lh[rows, :], ll[rows, :] = split(two)

    for b, at in enumerate(from_col):
        for pair in range(col_sets // 2):
            two = jnp.concatenate([right[2 * pair][at], right[2 * pair + 1][at]], axis=0)
            rows = pl.ds(b * depth + pair * 16, 16)
            rh[rows, :], rl[rows, :] = split(two)

    dims = (((0,), (0,)), ((), ()))
    dot = functools.partial(lax.dot_general, dimension_numbers=dims, preferred_element_type=jnp.float32)
    total = dot(lh[...], rh[...]) + dot(ll[...], rh[...]) + dot(lh[...], rl[...])
    out[...] = acc[...] + total * scale


def accumulate(acc, left, row_classes, where_c, right, where_r, place, scale):
    m, n = acc.shape
    tile = min(TILE_N, n)
    k = 8 * len(right) * len(row_classes)
    grid_spec = pltpu.PrefetchScalarGridSpec(
        num_scalar_prefetch=1,
        grid=(n // tile,),
        in_specs=[pl.BlockSpec((m, tile), lambda j, t: (0, j))]
        + [pl.BlockSpec(v.shape, lambda j, t: (0, 0, 0), pipeline_mode=pl.Buffered(1)) for v in left]
        + [pl.BlockSpec((v.shape[0], 8, tile), lambda j, t: (0, 0, j)) for v in right],
        out_specs=pl.BlockSpec((m, tile), lambda j, t: (0, j)),
        scratch_shapes=[pltpu.VMEM((k, m), jnp.bfloat16)] * 2 + [pltpu.VMEM((k, tile), jnp.bfloat16)] * 2,
    )
    return pl.pallas_call(
        functools.partial(kernel, row_classes, where_c, where_r, len(left), scale),
        out_shape=jax.ShapeDtypeStruct(acc.shape, acc.dtype),
        grid_spec=grid_spec,
        cost_estimate=pl.CostEstimate(flops=6 * m * n * k, bytes_accessed=4 * k * (m + n) + 8 * m * n, transcendentals=0),
        compiler_params=pltpu.CompilerParams(vmem_limit_bytes=56 << 20),
    )(place, acc, *left, *right)


def step(fisher, slab):
    n_row, n_col = lax.axis_size("row"), lax.axis_size("col")
    rows, order = slab.shape
    t_row, t_col = order // n_row, order // n_col
    scale = 1.0 / (rows * n_row * n_col)
    place = jnp.stack([lax.axis_index("row"), lax.axis_index("col")])

    def exchange(axis, n, t, slab):
        got = lax.all_to_all(slab.reshape(rows, n, t), axis, split_axis=1, concat_axis=1, tiled=True)
        return got.transpose(1, 0, 2)

    s = exchange("row", n_row, t_row, slab)
    xp, xm, x2 = send(s, dx=1), send(s, dx=-1), send(s, dx=2)
    zp, zm = send(s, dzh=1), send(s, dzh=-1)
    d = exchange("col", n_col, t_col, slab)
    z2 = send(s, dzh=2)
    b = jnp.concatenate([zp, zm], axis=0)
    bp, bm = send(b, dx=1), send(b, dx=-1)
    b2p, b2m = send(bp[:16], dx=1), send(bm[16:], dx=-1)
    cp, cm = send(z2, dx=1), send(z2, dx=-1)
    c2p, c2m = send(cp[:8], dx=1), send(cm[8:], dx=-1)

    dl = send(d, dzl=1)
    dp, dm = send(d, dy=1), send(d, dy=-1)
    lp, lm = send(dl, dy=1), send(dl, dy=-1)
    d2, l2 = send(dp, dy=1), send(lm, dy=-1)
    own = [(d, 0, 0), (dl, 0, 1), (dp, 1, 0), (dm, -1, 0), (lp, 1, 1), (lm, -1, 1), (d2, 2, 0), (l2, 2, 1)]
    right, where_r = [], []
    for value, dy, dzl in own:
        right += [value, send(value, dk=1)]
        where_r += [(dy, dzl, 0), (dy, dzl, 1)]

    def add(acc, left, row_classes, where_c):
        return accumulate(acc, left, row_classes, where_c, right, where_r, place, scale)

    acc = add(
        fisher,
        [s, xp, xm, x2, b, z2, bp, bm],
        [(0, 0), (1, 0), (2, 0), (3, 0), (4, 0), (4, 16), (5, 0), (6, 0), (6, 16), (7, 0), (7, 16)],
        [(0, 0), (1, 0), (-1, 0), (2, 0), (0, 1), (0, -1), (0, 2), (1, 1), (1, -1), (-1, 1), (-1, -1)],
    )
    acc = add(acc, [b2p, b2m, cp, cm], [(0, 0), (1, 0), (2, 0), (3, 0)], [(2, 1), (2, -1), (1, 2), (-1, 2)])
    acc, c2p, c2m = lax.optimization_barrier((acc, c2p, c2m))
    return add(acc, [jnp.concatenate([c2p, c2m], axis=0)], [(0, 0)], [(2, 2)])


def solution(mesh):
    return jax.shard_map(
        step,
        mesh=mesh,
        in_specs=(P("row", "col"), P(("row", "col"), None)),
        out_specs=P("row", "col"),
        check_vma=False,
    )
```

time: 259 us -> 198 us (0.76); the launches traced: 259 us -> 195 us
  waiting for transfers between devices: 144 us -> 85.1 us
  matrix products: 45 us -> 0 us
  starting transfers between devices: 0.04 us -> 41.9 us
  Pallas kernels: 0 us -> 34.6 us
  blocking collectives: 44.5 us -> 24.9 us
  between operations: 13.4 us -> 0.4 us
  local copies, waits for them, and re-layouts: 11.5 us -> 6.45 us
    all_gather x2 -> x0, waiting for transfers between devices: 144 us -> none  [the longest x1 106 us: row_panel(): lax.all_gather(pieces.reshape(rows, n_row, 1, t_row), 'col', axis=2, tile...]
    ppermute x0 -> x29, waiting for transfers between devices: none -> 75.4 us  [send(): return lax.ppermute(value, AXES, pairs)]
    dot_general x1 -> x0, matrix products: 45 us -> none  [transposed_product(): lax.dot_general(left, right, (((0, 1, 2), (0, 1, 2)), ((), ())), precisio...]
    pallas_call x0 -> x3, Pallas kernels: none -> 34.6 us  [accumulate(): pl.pallas_call(functools.partial(kernel, row_classes, where_c, where_r, l...]
    ppermute x0 -> x29, starting transfers between devices: none -> 33.8 us  [send(): return lax.ppermute(value, AXES, pairs)]
    all_to_all x2 -> x1, blocking collectives: 44.5 us -> 24.9 us  [exchange(): lax.all_to_all(slab.reshape(rows, n, t), axis, split_axis=1, concat_axis=...]
    all_gather x1 -> x0, local copies, waits for them, and re-layouts: 11.5 us -> none  [direct_product(): lax.all_gather(local_right, 'row', axis=1, tiled=True)]
    all_to_all x0 -> x1, waiting for transfers between devices: none -> 9.69 us  [exchange(): lax.all_to_all(slab.reshape(rows, n, t), axis, split_axis=1, concat_axis=...]
  transfers between devices with their start and end apart: 2 -> 30, of which waited for: 2 -> 9; matrix products, arithmetic and copies ran while one was open for 4% -> 2% of each run, Pallas kernels for 0% -> 14%
where the time goes in v1:
time: 198 us; the launch traced here: 195 us
  waiting for transfers between devices  85.1 us (43%)
  starting transfers between devices  41.9 us (21%)
  Pallas kernels  34.6 us (17%)
  blocking collectives  24.9 us (13%)
  local copies, waits for them, and re-layouts  6.45 us (3%)
    ppermute x29, waiting for transfers between devices, send(): return lax.ppermute(value, AXES, pairs)  75.4 us
    pallas_call x3, Pallas kernels, accumulate(): pl.pallas_call(functools.partial(kernel, row_classes, where_c, where_r, l...  34.6 us
    ppermute x29, starting transfers between devices, send(): return lax.ppermute(value, AXES, pairs)  33.8 us
    all_to_all x1, blocking collectives, exchange(): lax.all_to_all(slab.reshape(rows, n, t), axis, split_axis=1, concat_axis=...  24.9 us
    all_to_all x1, waiting for transfers between devices, exchange(): lax.all_to_all(slab.reshape(rows, n, t), axis, split_axis=1, concat_axis=...  9.69 us
    all_to_all x1, starting transfers between devices, exchange(): lax.all_to_all(slab.reshape(rows, n, t), axis, split_axis=1, concat_axis=...  8.04 us
  transfers between devices with their start and end apart: 30, of which 9 were waited for; matrix products, arithmetic and copies ran while one was open for 2% of the time, Pallas kernels for 14%

profile of v1, /device:TPU:37, one launch (start us, length us, event | category | flops | bytes accessed | tf_op | source)
XLA Modules:
  0.0 194.8 jit_solution(7782823487568707631)
XLA Ops:
  0.0 24.9 %all_to_all.10 = f32[8,16,1024]{2,0,1:T(8,128)S(1)} all-to-all(f32[8,16,1024]{2,0,1:T(8,128)} %bitcast.12), channel_id=1, replica_groups=mesh['row'=16,'col'=16] {'col'}, dimensions={1} | all-to-all | bytes 1048576 | tf_op jit(solution)/shard_map/all_to_all | solution.py:93
  24.9 8.0 %all-to-all-start = ((f32[8,16,1024]{2,0,1:T(8,128)}), f32[8,16,1024]{2,0,1:T(8,128)}, u32[]{:S(2)}, u32[]{:S(2)}) async-start(f32[8,16,1024]{2,0,1:T(8,128)} %bitcast.13), calls=%async_computation | async-start | bytes 1048576 | tf_op jit(solution)/shard_map/all_to_all | solution.py:93
  33.0 0.1 collective-permute-start.9
  33.1 9.7 %all-to-all-done = f32[8,16,1024]{2,0,1:T(8,128)} async-done(((f32[8,16,1024]{2,0,1:T(8,128)}), f32[8,16,1024]{2,0,1:T(8,128)}, u32[]{:S(2)}, u32[]{:S(2)}) %all-to-all-start) | async-done | bytes 524320 | tf_op jit(solution)/shard_map/all_to_all | solution.py:93
  42.8 1.2 collective-permute-start.3
  44.0 1.2 collective-permute-start.4
  45.1 0.1 collective-permute-start.11
  45.2 1.4 collective-permute-start.13
  46.6 15.9 %collective-permute-done.9.refs_10_.refs_6_.refs_3_ = f32[16,8,1024]{2,1,0:T(8,128)S(1)} collective-permute-done((f32[16,8,1024]{2,1,0:T(8,128)S(1)}, f32[16,8,1024]{2,1,0:T(8,128)S(1)}, u32[]{:S(2)}, u32[]{:S(2)}) %collective-permute-start.9) | collective-permute-done | bytes 524320 | tf_op jit(solution)/shard_map/ppermute | solution.py:26
  62.5 1.2 collective-permute-start.5
  63.6 10.1 %collective-permute-done.3 = f32[16,8,1024]{2,1,0:T(8,128)S(1)} collective-permute-done((f32[16,8,1024]{2,1,0:T(8,128)}, f32[16,8,1024]{2,1,0:T(8,128)S(1)}, u32[]{:S(2)}, u32[]{:S(2)}) %collective-permute-start.3) | collective-permute-done | bytes 524320 | tf_op jit(solution)/shard_map/ppermute | solution.py:26
  73.7 2.1 %collective-permute-start.8 = (f32[16,8,1024]{2,1,0:T(8,128)S(1)}, f32[16,8,1024]{2,1,0:T(8,128)S(1)}, u32[]{:S(2)}, u32[]{:S(2)}) collective-permute-start(f32[16,8,1024]{2,1,0:T(8,128)S(1)} %bitcast.8), channel_id=1, source_target_pairs={{16,0},{17,1},{18,2},{19,3},{20,4},{21,5},{22,6},{23,7},{24,8},{25... | collective-permute-start | bytes 1572872 | tf_op jit(solution)/shard_map/ppermute | solution.py:26
  75.8 0.0 collective-permute-done.4
  75.8 0.1 collective-permute-start
  75.9 1.8 collective-permute-start.1
  77.8 3.3 %collective-permute-start.2 = (f32[16,8,1024]{2,1,0:T(8,128)}, f32[16,8,1024]{2,1,0:T(8,128)S(1)}, u32[]{:S(2)}, u32[]{:S(2)}) collective-permute-start(f32[16,8,1024]{2,1,0:T(8,128)} %bitcast.3.refs_0_), channel_id=1, source_target_pairs={{8,0},{9,1},{10,2},{11,3},{12,4},{13,5},{14,6},{15,7},{0,8},{1,9},... | collective-permute-start | bytes 1572872 | tf_op jit(solution)/shard_map/ppermute | solution.py:26
  81.0 15.8 %collective-permute-done.5.refs_5_ = f32[16,8,1024]{2,1,0:T(8,128)S(1)} collective-permute-done((f32[16,8,1024]{2,1,0:T(8,128)}, f32[16,8,1024]{2,1,0:T(8,128)S(1)}, u32[]{:S(2)}, u32[]{:S(2)}) %collective-permute-start.5) | collective-permute-done | bytes 524320 | tf_op jit(solution)/shard_map/ppermute | solution.py:26
  96.8 1.2 collective-permute-start.17
  98.0 0.0 collective-permute-done.8.refs_9_.refs_5_.refs_2_
  98.0 1.5 collective-permute-start.15
  99.6 0.0 collective-permute-done.refs_1_
  99.6 1.3 collective-permute-start.19
  100.9 0.0 collective-permute-done.1.refs_2_
  100.9 1.8 collective-permute-start.10
  102.7 1.5 collective-permute-done.2.refs_3_
  104.2 6.3 %collective-permute-done.17.refs_18_.refs_14_.refs_11_ = f32[16,8,1024]{2,1,0:T(8,128)S(1)} collective-permute-done((f32[16,8,1024]{2,1,0:T(8,128)S(1)}, f32[16,8,1024]{2,1,0:T(8,128)S(1)}, u32[]{:S(2)}, u32[]{:S(2)}) %collective-permute-start.17) | collective-permute-done | bytes 524320 | tf_op jit(solution)/shard_map/ppermute | solution.py:26
  110.5 1.0 collective-permute-start.7
  111.5 2.7 %collective-permute-start.12 = (f32[16,8,1024]{2,1,0:T(8,128)S(1)}, f32[16,8,1024]{2,1,0:T(8,128)S(1)}, u32[]{:S(2)}, u32[]{:S(2)}) collective-permute-start(f32[16,8,1024]{2,1,0:T(8,128)S(1)} %collective-permute-done.11.refs_12_.refs_8_.refs_5_), channel_id=1, source_target_pairs={{16,0},{17,1},{18,2},{19,3},{20,4},{21,5},{22,6},{23,7},{24,8},{25... | collective-permute-start | bytes 1572872 | tf_op jit(solution)/shard_map/ppermute | solution.py:26
  114.2 7.4 %collective-permute-done.19.refs_20_.refs_16_.refs_13_ = f32[16,8,1024]{2,1,0:T(8,128)} collective-permute-done((f32[16,8,1024]{2,1,0:T(8,128)S(1)}, f32[16,8,1024]{2,1,0:T(8,128)}, u32[]{:S(2)}, u32[]{:S(2)}) %collective-permute-start.19) | collective-permute-done | bytes 524320 | tf_op jit(solution)/shard_map/ppermute | solution.py:26
  121.6 0.8 collective-permute-start.25
  122.4 0.0 collective-permute-done.10.refs_11_.refs_7_.refs_4_
  122.4 0.6 collective-permute-start.26
  123.0 0.0 collective-permute-done.12.refs_13_.refs_9_.refs_6_
  123.1 1.2 collective-permute-start.21
  124.2 14.8 %collective-permute-done.25.refs_2_ = f32[16,8,1024]{2,1,0:T(8,128)S(1)} collective-permute-done((f32[16,8,1024]{2,1,0:T(8,128)S(1)}, f32[16,8,1024]{2,1,0:T(8,128)S(1)}, u32[]{:S(2)}, u32[]{:S(2)}) %collective-permute-start.25) | collective-permute-done | bytes 524320 | tf_op jit(solution)/shard_map/ppermute | solution.py:26
  139.0 2.0 %collective-permute-start.14 = (f32[16,8,1024]{2,1,0:T(8,128)S(1)}, f32[16,8,1024]{2,1,0:T(8,128)}, u32[]{:S(2)}, u32[]{:S(2)}) collective-permute-start(f32[16,8,1024]{2,1,0:T(8,128)S(1)} %collective-permute-done.13.refs_14_.refs_10_.refs_7_), channel_id=1, source_target_pairs={{16,0},{17,1},{18,2},{19,3},{20,4},{21,5},{22,6},{23,7},{24,8},{25... | collective-permute-start | bytes 1572872 | tf_op jit(solution)/shard_map/ppermute | solution.py:26
  141.0 3.6 %collective-permute-done.26.refs_3_ = f32[16,8,1024]{2,1,0:T(8,128)S(1)} collective-permute-done((f32[16,8,1024]{2,1,0:T(8,128)S(1)}, f32[16,8,1024]{2,1,0:T(8,128)S(1)}, u32[]{:S(2)}, u32[]{:S(2)}) %collective-permute-start.26) | collective-permute-done | bytes 524320 | tf_op jit(solution)/shard_map/ppermute | solution.py:26
  144.7 2.7 %collective-permute-start.18 = (f32[16,8,1024]{2,1,0:T(8,128)S(1)}, f32[16,8,1024]{2,1,0:T(8,128)}, u32[]{:S(2)}, u32[]{:S(2)}) collective-permute-start(f32[16,8,1024]{2,1,0:T(8,128)S(1)} %collective-permute-done.17.refs_18_.refs_14_.refs_11_), channel_id=1, source_target_pairs={{16,0},{17,1},{18,2},{19,3},{20,4},{21,5},{22,6},{23,7},{24,8},{25... | collective-permute-start | bytes 1572872 | tf_op jit(solution)/shard_map/ppermute | solution.py:26
  147.4 0.1 collective-permute-start.16
  147.5 0.0 collective-permute-done.7.refs_7_
  147.5 0.4 collective-permute-start.20
  147.9 0.0 collective-permute-done.21.refs_22_.refs_18_.refs_15_
  147.9 0.1 collective-permute-start.22
  148.0 0.3 copy-done.12
  148.4 0.3 copy-done.13
  148.7 0.6 pad_add_fusion.place
  149.2 1.0 slice.18
  150.2 1.0 slice.19
  151.2 1.1 slice.16
  152.3 1.1 slice.17
  153.4 0.9 collective-permute-start.27
  154.3 0.0 collective-permute-done.18.refs_19_.refs_15_.refs_12_
  154.3 0.6 collective-permute-start.28
  154.9 0.0 collective-permute-done.16.refs_17_.refs_13_.refs_10_
  154.9 1.6 collective-permute-start.23
  156.5 0.9 collective-permute-start.24
  157.5 17.4 %shard_map.28.acc = f32[1024,1024]{1,0:T(8,128)} custom-call(s32[2]{0:T(128)} %pad_add_fusion.place, f32[1024,1024]{1,0:T(8,128)} %acc.1, f32[16,8,1024]{2,1,0:T(8,128)} %bitcast.3.refs_0_, f32[16,8,1024]{2,1,0:T(8,128)} %copy-done.16, f32[16,8,1024]{2,1,0:T(8,128)} %copy-done.17, f32[16,8,1024]{2,1,0:T(8,128)} %copy-done.18, f32[32,8,1024]{2,1,0:T(8,128)} %copy-done.14, ...), custom_call_target="tpu_custom_call" | custom-call | flops 8858370048 | bytes 19922944 | tf_op jit(solution)/shard_map/pallas_call | solution.py:76
  174.9 0.0 collective-permute-done.24.refs_1_
  175.0 0.8 copy-done.10
  175.7 0.8 copy-done.11
  176.5 9.5 %shard_map.29.acc = f32[1024,1024]{1,0:T(8,128)} custom-call(s32[2]{0:T(128)} %pad_add_fusion.place, f32[1024,1024]{1,0:T(8,128)} %shard_map.28.acc, f32[16,8,1024]{2,1,0:T(8,128)} %copy-done.10, f32[16,8,1024]{2,1,0:T(8,128)} %copy-done.11, f32[16,8,1024]{2,1,0:T(8,128)} %copy-done.8, f32[16,8,1024]{2,1,0:T(8,128)} %copy-done.9, f32[16,8,1024]{2,1,0:T(8,128)} %bitcast.10, ...), custom_call_target="tpu_custom_call" | custom-call | flops 3221225472 | bytes 12582912 | tf_op jit(solution)/shard_map/pallas_call | solution.py:76
  186.0 0.0 collective-permute-done.27
  186.0 0.8 pad_maximum_fusion.refs_0_
  186.9 7.7 %shard_map.30 = f32[1024,1024]{1,0:T(8,128)} custom-call(s32[2]{0:T(128)} %pad_add_fusion.place, f32[1024,1024]{1,0:T(8,128)} %shard_map.29.acc, f32[16,8,1024]{2,1,0:T(8,128)} %pad_maximum_fusion.refs_0_, f32[16,8,1024]{2,1,0:T(8,128)} %bitcast.11, f32[16,8,1024]{2,1,0:T(8,128)} %copy-done.4, f32[16,8,1024]{2,1,0:T(8,128)} %copy-done.1, ...), custom_call_target="tpu_custom_call" | custom-call | flops 805306368 | bytes 9437184 | tf_op jit(solution)/shard_map/pallas_call | solution.py:76
  (46 shorter events, 0.2 us)
Async XLA Ops:
  24.9 132.5 %copy-start = (f32[8,16,1024]{2,0,1:T(8,128)}, f32[8,16,1024]{2,0,1:T(8,128)S(1)}, u32[]{:S(2)}) copy-start(f32[8,16,1024]{2,0,1:T(8,128)S(1)} %all_to_all.10) | copy-start | bytes 1572868
  24.9 17.8 %all-to-all-start = ((f32[8,16,1024]{2,0,1:T(8,128)}), f32[8,16,1024]{2,0,1:T(8,128)}, u32[]{:S(2)}, u32[]{:S(2)}) async-start(f32[8,16,1024]{2,0,1:T(8,128)} %bitcast.13), calls=%async_computation | async-start | bytes 1048576 | tf_op jit(solution)/shard_map/all_to_all | solution.py:93
  33.0 29.5 %collective-permute-start.9 = (f32[16,8,1024]{2,1,0:T(8,128)S(1)}, f32[16,8,1024]{2,1,0:T(8,128)S(1)}, u32[]{:S(2)}, u32[]{:S(2)}) collective-permute-start(f32[16,8,1024]{2,1,0:T(8,128)S(1)} %bitcast.5), channel_id=1, source_target_pairs={{32,0},{33,1},{34,2},{35,3},{36,4},{37,5},{38,6},{39,7},{40,8},{41... | collective-permute-start | bytes 1572872 | tf_op jit(solution)/shard_map/ppermute | solution.py:26
  42.8 31.0 %collective-permute-start.3 = (f32[16,8,1024]{2,1,0:T(8,128)}, f32[16,8,1024]{2,1,0:T(8,128)S(1)}, u32[]{:S(2)}, u32[]{:S(2)}) collective-permute-start(f32[16,8,1024]{2,1,0:T(8,128)} %bitcast.3.refs_0_), channel_id=1, source_target_pairs={{1,0},{2,1},{3,2},{0,3},{5,4},{6,5},{7,6},{4,7},{9,8},{10,9},{11,1... | collective-permute-start | bytes 1572872 | tf_op jit(solution)/shard_map/ppermute | solution.py:26
  44.0 31.8 %collective-permute-start.4 = (f32[16,8,1024]{2,1,0:T(8,128)}, f32[16,8,1024]{2,1,0:T(8,128)S(1)}, u32[]{:S(2)}, u32[]{:S(2)}) collective-permute-start(f32[16,8,1024]{2,1,0:T(8,128)} %bitcast.3.refs_0_), channel_id=1, source_target_pairs={{3,0},{0,1},{1,2},{2,3},{7,4},{4,5},{5,6},{6,7},{11,8},{8,9},{9,10... | collective-permute-start | bytes 1572872 | tf_op jit(solution)/shard_map/ppermute | solution.py:26
  45.1 30.8 %collective-permute-start.11 = (f32[16,8,1024]{2,1,0:T(8,128)S(1)}, f32[16,8,1024]{2,1,0:T(8,128)S(1)}, u32[]{:S(2)}, u32[]{:S(2)}) collective-permute-start(f32[16,8,1024]{2,1,0:T(8,128)S(1)} %bitcast.6), channel_id=1, source_target_pairs={{64,0},{65,1},{66,2},{67,3},{68,4},{69,5},{70,6},{71,7},{72,8},{73... | collective-permute-start | bytes 1572872 | tf_op jit(solution)/shard_map/ppermute | solution.py:26
  45.2 32.6 %collective-permute-start.13 = (f32[16,8,1024]{2,1,0:T(8,128)S(1)}, f32[16,8,1024]{2,1,0:T(8,128)S(1)}, u32[]{:S(2)}, u32[]{:S(2)}) collective-permute-start(f32[16,8,1024]{2,1,0:T(8,128)S(1)} %bitcast.7), channel_id=1, source_target_pairs={{192,0},{193,1},{194,2},{195,3},{196,4},{197,5},{198,6},{199,7},{2... | collective-permute-start | bytes 1572872 | tf_op jit(solution)/shard_map/ppermute | solution.py:26
  62.5 95.0 %copy-start.1 = (f32[16,8,1024]{2,1,0:T(8,128)}, f32[16,8,1024]{2,1,0:T(8,128)S(1)}, u32[]{:S(2)}) copy-start(f32[16,8,1024]{2,1,0:T(8,128)S(1)} %collective-permute-done.9.refs_10_.refs_6_.refs_3_) | copy-start | bytes 1572868
  62.5 34.4 %collective-permute-start.5 = (f32[16,8,1024]{2,1,0:T(8,128)}, f32[16,8,1024]{2,1,0:T(8,128)S(1)}, u32[]{:S(2)}, u32[]{:S(2)}) collective-permute-start(f32[16,8,1024]{2,1,0:T(8,128)} %bitcast.3.refs_0_), channel_id=1, source_target_pairs={{2,0},{3,1},{0,2},{1,3},{6,4},{7,5},{4,6},{5,7},{10,8},{11,9},{8,1... | collective-permute-start | bytes 1572872 | tf_op jit(solution)/shard_map/ppermute | solution.py:26
  73.7 24.3 %collective-permute-start.8 = (f32[16,8,1024]{2,1,0:T(8,128)S(1)}, f32[16,8,1024]{2,1,0:T(8,128)S(1)}, u32[]{:S(2)}, u32[]{:S(2)}) collective-permute-start(f32[16,8,1024]{2,1,0:T(8,128)S(1)} %bitcast.8), channel_id=1, source_target_pairs={{16,0},{17,1},{18,2},{19,3},{20,4},{21,5},{22,6},{23,7},{24,8},{25... | collective-permute-start | bytes 1572872 | tf_op jit(solution)/shard_map/ppermute | solution.py:26
  75.8 23.8 %collective-permute-start = (f32[16,8,1024]{2,1,0:T(8,128)}, f32[16,8,1024]{2,1,0:T(8,128)S(1)}, u32[]{:S(2)}, u32[]{:S(2)}) collective-permute-start(f32[16,8,1024]{2,1,0:T(8,128)} %bitcast.3.refs_0_), channel_id=1, source_target_pairs={{4,0},{5,1},{6,2},{7,3},{8,4},{9,5},{10,6},{11,7},{12,8},{13,9},{1... | collective-permute-start | bytes 1572872 | tf_op jit(solution)/shard_map/ppermute | solution.py:26
  75.9 81.5 %copy-start.2 = (f32[16,8,1024]{2,1,0:T(8,128)}, f32[16,8,1024]{2,1,0:T(8,128)S(1)}, u32[]{:S(2)}) copy-start(f32[16,8,1024]{2,1,0:T(8,128)S(1)} %collective-permute-done.11.refs_12_.refs_8_.refs_5_) | copy-start | bytes 1572868
  75.9 25.0 %collective-permute-start.1 = (f32[16,8,1024]{2,1,0:T(8,128)}, f32[16,8,1024]{2,1,0:T(8,128)S(1)}, u32[]{:S(2)}, u32[]{:S(2)}) collective-permute-start(f32[16,8,1024]{2,1,0:T(8,128)} %bitcast.3.refs_0_), channel_id=1, source_target_pairs={{12,0},{13,1},{14,2},{15,3},{0,4},{1,5},{2,6},{3,7},{4,8},{5,9},{6... | collective-permute-start | bytes 1572872 | tf_op jit(solution)/shard_map/ppermute | solution.py:26
  77.8 79.7 %copy-start.3 = (f32[16,8,1024]{2,1,0:T(8,128)}, f32[16,8,1024]{2,1,0:T(8,128)S(1)}, u32[]{:S(2)}) copy-start(f32[16,8,1024]{2,1,0:T(8,128)S(1)} %collective-permute-done.13.refs_14_.refs_10_.refs_7_) | copy-start | bytes 1572868
  77.8 26.5 %collective-permute-start.2 = (f32[16,8,1024]{2,1,0:T(8,128)}, f32[16,8,1024]{2,1,0:T(8,128)S(1)}, u32[]{:S(2)}, u32[]{:S(2)}) collective-permute-start(f32[16,8,1024]{2,1,0:T(8,128)} %bitcast.3.refs_0_), channel_id=1, source_target_pairs={{8,0},{9,1},{10,2},{11,3},{12,4},{13,5},{14,6},{15,7},{0,8},{1,9},... | collective-permute-start | bytes 1572872 | tf_op jit(solution)/shard_map/ppermute | solution.py:26
  96.8 51.2 %copy-start.15 = (f32[16,8,1024]{2,1,0:T(8,128)}, f32[16,8,1024]{2,1,0:T(8,128)S(1)}, u32[]{:S(2)}) copy-start(f32[16,8,1024]{2,1,0:T(8,128)S(1)} %collective-permute-done.5.refs_5_) | copy-start | bytes 1572868
  96.8 13.7 %collective-permute-start.17 = (f32[16,8,1024]{2,1,0:T(8,128)S(1)}, f32[16,8,1024]{2,1,0:T(8,128)S(1)}, u32[]{:S(2)}, u32[]{:S(2)}) collective-permute-start(f32[16,8,1024]{2,1,0:T(8,128)S(1)} %collective-permute-done.9.refs_10_.refs_6_.refs_3_), channel_id=1, source_target_pairs={{192,0},{193,1},{194,2},{195,3},{196,4},{197,5},{198,6},{199,7},{2... | collective-permute-start | bytes 1572872 | tf_op jit(solution)/shard_map/ppermute | solution.py:26
  98.0 59.5 %copy-start.4 = (f32[16,8,1024]{2,1,0:T(8,128)}, f32[16,8,1024]{2,1,0:T(8,128)S(1)}, u32[]{:S(2)}) copy-start(f32[16,8,1024]{2,1,0:T(8,128)S(1)} %collective-permute-done.8.refs_9_.refs_5_.refs_2_) | copy-start | bytes 1572868
  98.0 13.5 %collective-permute-start.15 = (f32[16,8,1024]{2,1,0:T(8,128)S(1)}, f32[16,8,1024]{2,1,0:T(8,128)}, u32[]{:S(2)}, u32[]{:S(2)}) collective-permute-start(f32[16,8,1024]{2,1,0:T(8,128)S(1)} %collective-permute-done.9.refs_10_.refs_6_.refs_3_), channel_id=1, source_target_pairs={{64,0},{65,1},{66,2},{67,3},{68,4},{69,5},{70,6},{71,7},{72,8},{73... | collective-permute-start | bytes 1572872 | tf_op jit(solution)/shard_map/ppermute | solution.py:26
  99.6 48.4 %copy-start.14 = (f32[32,8,1024]{2,1,0:T(8,128)}, f32[32,8,1024]{2,1,0:T(8,128)S(1)}, u32[]{:S(2)}) copy-start(f32[32,8,1024]{2,1,0:T(8,128)S(1)} %constant_dynamic-update-slice_fusion.refs_4_) | copy-start | bytes 3145732
  99.6 48.4 %copy-start.16 = (f32[16,8,1024]{2,1,0:T(8,128)}, f32[16,8,1024]{2,1,0:T(8,128)S(1)}, u32[]{:S(2)}) copy-start(f32[16,8,1024]{2,1,0:T(8,128)S(1)} %collective-permute-done.refs_1_) | copy-start | bytes 1572868
  99.6 22.0 %collective-permute-start.19 = (f32[16,8,1024]{2,1,0:T(8,128)S(1)}, f32[16,8,1024]{2,1,0:T(8,128)}, u32[]{:S(2)}, u32[]{:S(2)}) collective-permute-start(f32[16,8,1024]{2,1,0:T(8,128)S(1)} %collective-permute-done.11.refs_12_.refs_8_.refs_5_), channel_id=1, source_target_pairs={{64,0},{65,1},{66,2},{67,3},{68,4},{69,5},{70,6},{71,7},{72,8},{73... | collective-permute-start | bytes 1572872 | tf_op jit(solution)/shard_map/ppermute | solution.py:26
  100.9 47.1 %copy-start.17 = (f32[16,8,1024]{2,1,0:T(8,128)}, f32[16,8,1024]{2,1,0:T(8,128)S(1)}, u32[]{:S(2)}) copy-start(f32[16,8,1024]{2,1,0:T(8,128)S(1)} %collective-permute-done.1.refs_2_) | copy-start | bytes 1572868
  100.9 21.5 %collective-permute-start.10 = (f32[16,8,1024]{2,1,0:T(8,128)S(1)}, f32[16,8,1024]{2,1,0:T(8,128)S(1)}, u32[]{:S(2)}, u32[]{:S(2)}) collective-permute-start(f32[16,8,1024]{2,1,0:T(8,128)S(1)} %collective-permute-done.9.refs_10_.refs_6_.refs_3_), channel_id=1, source_target_pairs={{16,0},{17,1},{18,2},{19,3},{20,4},{21,5},{22,6},{23,7},{24,8},{25... | collective-permute-start | bytes 1572872 | tf_op jit(solution)/shard_map/ppermute | solution.py:26
  104.2 43.8 %copy-start.18 = (f32[16,8,1024]{2,1,0:T(8,128)}, f32[16,8,1024]{2,1,0:T(8,128)S(1)}, u32[]{:S(2)}) copy-start(f32[16,8,1024]{2,1,0:T(8,128)S(1)} %collective-permute-done.2.refs_3_) | copy-start | bytes 1572868
  104.2 43.1 %collective-permute-start.6 = (f32[32,8,1024]{2,1,0:T(8,128)S(1)}, f32[32,8,1024]{2,1,0:T(8,128)S(1)}, u32[]{:S(2)}, u32[]{:S(2)}) collective-permute-start(f32[32,8,1024]{2,1,0:T(8,128)S(1)} %constant_dynamic-update-slice_fusion.refs_4_), channel_id=1, source_target_pairs={{4,0},{5,1},{6,2},{7,3},{8,4},{9,5},{10,6},{11,7},{12,8},{13,9},{1... | collective-permute-start | bytes 3145736 | tf_op jit(solution)/shard_map/ppermute | solution.py:26
  110.5 47.0 %copy-start.5 = (f32[16,8,1024]{2,1,0:T(8,128)}, f32[16,8,1024]{2,1,0:T(8,128)S(1)}, u32[]{:S(2)}) copy-start(f32[16,8,1024]{2,1,0:T(8,128)S(1)} %collective-permute-done.17.refs_18_.refs_14_.refs_11_) | copy-start | bytes 1572868
  110.5 36.9 %collective-permute-start.7 = (f32[32,8,1024]{2,1,0:T(8,128)S(1)}, f32[32,8,1024]{2,1,0:T(8,128)S(1)}, u32[]{:S(2)}, u32[]{:S(2)}) collective-permute-start(f32[32,8,1024]{2,1,0:T(8,128)S(1)} %constant_dynamic-update-slice_fusion.refs_4_), channel_id=1, source_target_pairs={{12,0},{13,1},{14,2},{15,3},{0,4},{1,5},{2,6},{3,7},{4,8},{5,9},{6... | collective-permute-start | bytes 3145736 | tf_op jit(solution)/shard_map/ppermute | solution.py:26
  111.5 11.6 %collective-permute-start.12 = (f32[16,8,1024]{2,1,0:T(8,128)S(1)}, f32[16,8,1024]{2,1,0:T(8,128)S(1)}, u32[]{:S(2)}, u32[]{:S(2)}) collective-permute-start(f32[16,8,1024]{2,1,0:T(8,128)S(1)} %collective-permute-done.11.refs_12_.refs_8_.refs_5_), channel_id=1, source_target_pairs={{16,0},{17,1},{18,2},{19,3},{20,4},{21,5},{22,6},{23,7},{24,8},{25... | collective-permute-start | bytes 1572872 | tf_op jit(solution)/shard_map/ppermute | solution.py:26
  121.6 17.5 %collective-permute-start.25 = (f32[16,8,1024]{2,1,0:T(8,128)S(1)}, f32[16,8,1024]{2,1,0:T(8,128)S(1)}, u32[]{:S(2)}, u32[]{:S(2)}) collective-permute-start(f32[16,8,1024]{2,1,0:T(8,128)S(1)} %collective-permute-done.5.refs_5_), channel_id=1, source_target_pairs={{4,0},{5,1},{6,2},{7,3},{8,4},{9,5},{10,6},{11,7},{12,8},{13,9},{1... | collective-permute-start | bytes 1572872 | tf_op jit(solution)/shard_map/ppermute | solution.py:26
  122.4 25.5 %copy-start.6 = (f32[16,8,1024]{2,1,0:T(8,128)}, f32[16,8,1024]{2,1,0:T(8,128)S(1)}, u32[]{:S(2)}) copy-start(f32[16,8,1024]{2,1,0:T(8,128)S(1)} %collective-permute-done.10.refs_11_.refs_7_.refs_4_) | copy-start | bytes 1572868
  122.4 22.3 %collective-permute-start.26 = (f32[16,8,1024]{2,1,0:T(8,128)S(1)}, f32[16,8,1024]{2,1,0:T(8,128)S(1)}, u32[]{:S(2)}, u32[]{:S(2)}) collective-permute-start(f32[16,8,1024]{2,1,0:T(8,128)S(1)} %collective-permute-done.5.refs_5_), channel_id=1, source_target_pairs={{12,0},{13,1},{14,2},{15,3},{0,4},{1,5},{2,6},{3,7},{4,8},{5,9},{6... | collective-permute-start | bytes 1572872 | tf_op jit(solution)/shard_map/ppermute | solution.py:26
  123.1 25.0 %copy-start.7 = (f32[16,8,1024]{2,1,0:T(8,128)}, f32[16,8,1024]{2,1,0:T(8,128)S(1)}, u32[]{:S(2)}) copy-start(f32[16,8,1024]{2,1,0:T(8,128)S(1)} %collective-permute-done.12.refs_13_.refs_9_.refs_6_) | copy-start | bytes 1572868
  123.1 24.8 %collective-permute-start.21 = (f32[16,8,1024]{2,1,0:T(8,128)S(1)}, f32[16,8,1024]{2,1,0:T(8,128)}, u32[]{:S(2)}, u32[]{:S(2)}) collective-permute-start(f32[16,8,1024]{2,1,0:T(8,128)S(1)} %collective-permute-done.17.refs_18_.refs_14_.refs_11_), channel_id=1, source_target_pairs={{192,0},{193,1},{194,2},{195,3},{196,4},{197,5},{198,6},{199,7},{2... | collective-permute-start | bytes 1572872 | tf_op jit(solution)/shard_map/ppermute | solution.py:26
  139.0 9.0 %copy-start.8 = (f32[16,8,1024]{2,1,0:T(8,128)}, f32[16,8,1024]{2,1,0:T(8,128)S(1)}, u32[]{:S(2)}) copy-start(f32[16,8,1024]{2,1,0:T(8,128)S(1)} %collective-permute-done.25.refs_2_) | copy-start | bytes 1572868
  139.0 14.3 %collective-permute-start.14 = (f32[16,8,1024]{2,1,0:T(8,128)S(1)}, f32[16,8,1024]{2,1,0:T(8,128)}, u32[]{:S(2)}, u32[]{:S(2)}) collective-permute-start(f32[16,8,1024]{2,1,0:T(8,128)S(1)} %collective-permute-done.13.refs_14_.refs_10_.refs_7_), channel_id=1, source_target_pairs={{16,0},{17,1},{18,2},{19,3},{20,4},{21,5},{22,6},{23,7},{24,8},{25... | collective-permute-start | bytes 1572872 | tf_op jit(solution)/shard_map/ppermute | solution.py:26
  144.7 3.4 %copy-start.9 = (f32[16,8,1024]{2,1,0:T(8,128)}, f32[16,8,1024]{2,1,0:T(8,128)S(1)}, u32[]{:S(2)}) copy-start(f32[16,8,1024]{2,1,0:T(8,128)S(1)} %collective-permute-done.26.refs_3_) | copy-start | bytes 1572868
  144.7 9.6 %collective-permute-start.18 = (f32[16,8,1024]{2,1,0:T(8,128)S(1)}, f32[16,8,1024]{2,1,0:T(8,128)}, u32[]{:S(2)}, u32[]{:S(2)}) collective-permute-start(f32[16,8,1024]{2,1,0:T(8,128)S(1)} %collective-permute-done.17.refs_18_.refs_14_.refs_11_), channel_id=1, source_target_pairs={{16,0},{17,1},{18,2},{19,3},{20,4},{21,5},{22,6},{23,7},{24,8},{25... | collective-permute-start | bytes 1572872 | tf_op jit(solution)/shard_map/ppermute | solution.py:26
  147.4 1.0 copy-start.12
  147.4 7.6 %collective-permute-start.16 = (f32[16,8,1024]{2,1,0:T(8,128)}, f32[16,8,1024]{2,1,0:T(8,128)}, u32[]{:S(2)}, u32[]{:S(2)}) collective-permute-start(f32[16,8,1024]{2,1,0:T(8,128)} %collective-permute-done.15.refs_16_.refs_12_.refs_9_), channel_id=1, source_target_pairs={{16,0},{17,1},{18,2},{19,3},{20,4},{21,5},{22,6},{23,7},{24,8},{25... | collective-permute-start | bytes 1572872 | tf_op jit(solution)/shard_map/ppermute | solution.py:26
  147.5 1.2 copy-start.13
  147.5 9.1 %collective-permute-start.20 = (f32[16,8,1024]{2,1,0:T(8,128)}, f32[16,8,1024]{2,1,0:T(8,128)}, u32[]{:S(2)}, u32[]{:S(2)}) collective-permute-start(f32[16,8,1024]{2,1,0:T(8,128)} %collective-permute-done.19.refs_20_.refs_16_.refs_13_), channel_id=1, source_target_pairs={{16,0},{17,1},{18,2},{19,3},{20,4},{21,5},{22,6},{23,7},{24,8},{25... | collective-permute-start | bytes 1572872 | tf_op jit(solution)/shard_map/ppermute | solution.py:26
  147.9 9.6 %collective-permute-start.22 = (f32[16,8,1024]{2,1,0:T(8,128)}, f32[16,8,1024]{2,1,0:T(8,128)}, u32[]{:S(2)}, u32[]{:S(2)}) collective-permute-start(f32[16,8,1024]{2,1,0:T(8,128)} %collective-permute-done.21.refs_22_.refs_18_.refs_15_), channel_id=1, source_target_pairs={{16,0},{17,1},{18,2},{19,3},{20,4},{21,5},{22,6},{23,7},{24,8},{25... | collective-permute-start | bytes 1572872 | tf_op jit(solution)/shard_map/ppermute | solution.py:26
  153.4 32.7 %collective-permute-start.27 = (f32[8,8,1024]{2,1,0:T(8,128)S(1)}, f32[8,8,1024]{2,1,0:T(8,128)S(1)}, u32[]{:S(2)}, u32[]{:S(2)}) collective-permute-start(f32[8,8,1024]{2,1,0:T(8,128)S(1)} %slice.18), channel_id=1, source_target_pairs={{4,0},{5,1},{6,2},{7,3},{8,4},{9,5},{10,6},{11,7},{12,8},{13,9},{1... | collective-permute-start | bytes 786440 | tf_op jit(solution)/shard_map/ppermute | solution.py:26
  154.3 31.8 %collective-permute-start.28 = (f32[8,8,1024]{2,1,0:T(8,128)S(1)}, f32[8,8,1024]{2,1,0:T(8,128)S(1)}, u32[]{:S(2)}, u32[]{:S(2)}) collective-permute-start(f32[8,8,1024]{2,1,0:T(8,128)S(1)} %slice.19), channel_id=1, source_target_pairs={{12,0},{13,1},{14,2},{15,3},{0,4},{1,5},{2,6},{3,7},{4,8},{5,9},{6... | collective-permute-start | bytes 786440 | tf_op jit(solution)/shard_map/ppermute | solution.py:26
  154.9 20.0 %collective-permute-start.23 = (f32[16,8,1024]{2,1,0:T(8,128)S(1)}, f32[16,8,1024]{2,1,0:T(8,128)S(1)}, u32[]{:S(2)}, u32[]{:S(2)}) collective-permute-start(f32[16,8,1024]{2,1,0:T(8,128)S(1)} %slice.16), channel_id=1, source_target_pairs={{4,0},{5,1},{6,2},{7,3},{8,4},{9,5},{10,6},{11,7},{12,8},{13,9},{1... | collective-permute-start | bytes 1572872 | tf_op jit(solution)/shard_map/ppermute | solution.py:26
  156.5 18.4 %collective-permute-start.24 = (f32[16,8,1024]{2,1,0:T(8,128)S(1)}, f32[16,8,1024]{2,1,0:T(8,128)S(1)}, u32[]{:S(2)}, u32[]{:S(2)}) collective-permute-start(f32[16,8,1024]{2,1,0:T(8,128)S(1)} %slice.17), channel_id=1, source_target_pairs={{12,0},{13,1},{14,2},{15,3},{0,4},{1,5},{2,6},{3,7},{4,8},{5,9},{6... | collective-permute-start | bytes 1572872 | tf_op jit(solution)/shard_map/ppermute | solution.py:26
  174.9 0.8 copy-start.10
  175.7 0.8 copy-start.11

commit v2 on v0

v2 whole, which is shorter than its diff:
```python
import functools

import jax
import jax.numpy as jnp
from jax import lax
from jax.experimental import pallas as pl
from jax.experimental.pallas import tpu as pltpu
from jax.sharding import PartitionSpec as P


AXES = ("row", "col")
TILE_N = 512
VMEM_BYTES = 24 << 20
INSIDE = pl.BlockSpec(memory_space=pltpu.VMEM)

SOURCES = (
    [(0, 0), (1, 0), (-1, 0), (2, 0), (0, 1), (0, -1), (1, 1), (-1, 1), (1, -1), (-1, -1), (0, 2)],
    [(2, 1), (2, -1), (1, 2), (-1, 2)],
    [(2, 2)],
)

STEPS = (0, 1, -1, 2)


def send(value, dy=0, dzl=0, dk=0, dx=0, dzh=0):
    def of(offset, k):
        return offset[k] if isinstance(offset, tuple) else offset

    pairs = []
    for y in range(4):
        for zl in range(2):
            for k in range(2):
                for x in range(4):
                    for zh in range(4):
                        here = (y * 4 + zl * 2 + k) * 16 + x * 4 + zh
                        there = (((y + of(dy, k)) % 4) * 4 + (zl ^ dzl) * 2 + (k ^ dk)) * 16
                        there += ((x + of(dx, k)) % 4) * 4 + (zh + of(dzh, k)) % 4
                        pairs.append((there, here))
    return lax.ppermute(value, AXES, pairs)


def relay(plus, minus, axis):
    value = jnp.where(lax.axis_index("row") & 1 == 0, plus, minus)
    return send(value, **{axis: (1, -1)})


def exchange(slab, axis):
    rows, order = slab.shape
    n = lax.axis_size(axis)
    got = lax.all_to_all(slab.reshape(rows, n, order // n), axis, split_axis=1, concat_axis=1, tiled=True)
    return got.transpose(1, 0, 2)


def split(value):
    high = value.astype(jnp.bfloat16)
    return high, (value - high.astype(jnp.float32)).astype(jnp.bfloat16)


def prepare_kernel(place, *refs):
    pieces, outs = refs[:8], refs[8:]
    c = place[1]
    width = 256

    @pl.loop(0, pieces[0].shape[2] // width)
    def _(j):
        cols = pl.ds(pl.multiple_of(j * width, width), width)
        for group, sources in enumerate(SOURCES):
            high, low = outs[2 * group : 2 * group + 2]
            for b, (dx, dzh) in enumerate(sources):
                at = (((c >> 2) + dx) & 3) * 4 + (((c & 3) + dzh) & 3)
                for i in range(4):
                    rows = pl.ds(b * 64 + i * 16, 16)
                    both = jnp.concatenate([pieces[2 * i][at, :, cols], pieces[2 * i + 1][at, :, cols]], axis=0)
                    high[rows, cols], low[rows, cols] = split(both)


def prepare(pieces, place):
    m = pieces[0].shape[2]
    ks = [64 * len(sources) for sources in SOURCES for _ in range(2)]
    return pl.pallas_call(
        prepare_kernel,
        out_shape=[jax.ShapeDtypeStruct((k, m), jnp.bfloat16) for k in ks],
        in_specs=[pl.BlockSpec(memory_space=pltpu.SMEM)] + [INSIDE] * len(pieces),
        out_specs=[INSIDE] * len(ks),
        cost_estimate=pl.CostEstimate(flops=2 * sum(ks) * m, bytes_accessed=4 * sum(ks) * m, transcendentals=0),
        compiler_params=pltpu.CompilerParams(vmem_limit_bytes=VMEM_BYTES),
    )(place, *pieces)


def product_kernel(parts, n_left, scale, last, place, acc, *refs):
    left, right = refs[:n_left], refs[n_left : n_left + 2 * len(parts)]
    out, *scratch = refs[n_left + 2 * len(parts) :]
    m, n = acc.shape
    width = 256
    dims = (((0,), (0,)), ((), ()))
    dot = functools.partial(lax.dot_general, dimension_numbers=dims, preferred_element_type=jnp.float32)

    r = place[0]
    y, k = r >> 2, r & 1

    def pieces(cols):
        at = 0
        for half, classes in parts:
            zl = ((r >> 1) & 1) ^ half
            for which in classes:
                for dy in STEPS:
                    group = ((y + dy) & 3) * 4 + zl * 2
                    both = [left[which][group + (k ^ dk), :, cols] for dk in (0, 1)]
                    yield pl.ds(at, 16), jnp.concatenate(both, axis=0)
                    at += 16

    if not last:
        lh, ll = scratch

        @pl.loop(0, m // width)
        def _(j):
            cols = pl.ds(pl.multiple_of(j * width, width), width)
            for rows, value in pieces(cols):
                lh[rows, cols], ll[rows, cols] = split(value)

        @pl.loop(0, n // TILE_N)
        def _(j):
            cols = pl.ds(pl.multiple_of(j * TILE_N, TILE_N), TILE_N)
            at, total = 0, None
            for i in range(len(parts)):
                high, low = right[2 * i][:, cols], right[2 * i + 1][:, cols]
                rows = pl.ds(at, high.shape[0])
                at += high.shape[0]
                for term in (dot(lh[rows, :], high), dot(ll[rows, :], high), dot(lh[rows, :], low)):
                    total = term if total is None else total + term
            out[:, cols] = acc[:, cols] + total * scale

    else:
        ls, rs, held, sems = scratch
        depth = ls.shape[0] // 3
        for rows, value in pieces(slice(None)):
            high, low = split(value)
            for i, v in enumerate((high, low, high)):
                ls[pl.ds(i * depth + rows.start, 16), :] = v
        at = 0
        for i in range(len(parts)):
            size = right[2 * i].shape[0]
            for q, ref in enumerate((right[2 * i], right[2 * i], right[2 * i + 1])):
                rs[pl.ds(q * depth + at, size), :] = ref[...]
            at += size
        copies = []
        for j in range(n // TILE_N):
            cols = pl.ds(j * TILE_N, TILE_N)
            held[j] = acc[:, cols] + dot(ls[...], rs[:, cols]) * scale
            copies.append(pltpu.make_async_copy(held.at[j], out.at[:, cols], sems.at[j]))
            copies[-1].start()
        for copy in copies:
            copy.wait()


def add_product(acc, left, right, scale, place, last):
    m, n = acc.shape
    buffers, parts, rights = [], [], []
    for (half, group), classes in left.items():
        rights += right[half][2 * group : 2 * group + 2]
        for v in classes:
            if not any(v is u for u in buffers):
                buffers.append(v)
        parts.append((half, tuple(next(i for i, u in enumerate(buffers) if u is v) for v in classes)))
    total = sum(v.shape[0] for v in rights) // 2
    if last:
        tiles = n // TILE_N
        scratch = [pltpu.VMEM((3 * total, m), jnp.bfloat16), pltpu.VMEM((3 * total, n), jnp.bfloat16)]
        scratch += [pltpu.VMEM((tiles, m, TILE_N), jnp.float32), pltpu.SemaphoreType.DMA((tiles,))]
    else:
        scratch = [pltpu.VMEM((total, m), jnp.bfloat16)] * 2
    return pl.pallas_call(
        functools.partial(product_kernel, tuple(parts), len(buffers), scale, last),
        out_shape=jax.ShapeDtypeStruct(acc.shape, acc.dtype),
        in_specs=[pl.BlockSpec(memory_space=pltpu.SMEM)] + [INSIDE] * (1 + len(buffers) + len(rights)),
        out_specs=pl.BlockSpec(memory_space=pl.ANY) if last else INSIDE,
        scratch_shapes=scratch,
        cost_estimate=pl.CostEstimate(flops=6 * m * n * total, bytes_accessed=4 * total * (m + n) + 8 * m * n, transcendentals=0),
        compiler_params=pltpu.CompilerParams(vmem_limit_bytes=VMEM_BYTES),
    )(place, acc, *buffers, *rights)


def step(fisher, slab):
    scale = 1.0 / (slab.shape[0] * lax.axis_size("row") * lax.axis_size("col"))
    place = jnp.stack([lax.axis_index("row"), lax.axis_index("col")])

    s = exchange(slab, "row")
    d = exchange(slab, "col")
    zp, zm = send(s, dzh=1), send(s, dzh=-1)
    xp, xm = send(s, dx=1), send(s, dx=-1)
    x2 = relay(xp, xm, "dx")
    bpp, bmp = send(zp, dx=1), send(zp, dx=-1)
    bpm, bmm = send(zm, dx=1), send(zm, dx=-1)
    z2 = relay(zp, zm, "dzh")
    b2p, b2m = send(bpp, dx=1), send(bmm, dx=-1)
    cp, cm = send(z2, dx=1), send(z2, dx=-1)
    c2 = relay(cp, cm, "dx")

    dl = send(d, dzl=1)
    dp, dm = send(d, dy=1), send(d, dy=-1)
    lp, lm = send(dl, dy=1), send(dl, dy=-1)
    d2, l2 = relay(dp, dm, "dy"), relay(lp, lm, "dy")
    right = {}
    for half, own in enumerate([(d, dp, dm, d2), (dl, lp, lm, l2)]):
        pieces = []
        for value in own:
            pieces += [value, send(value, dk=1)]
        right[half] = prepare(pieces, place)

    first = [s, xp, xm, x2, zp, zm, bpp, bmp, bpm, bmm, z2]
    second = [b2p, b2m, cp, cm]
    third = [c2]
    calls = {
        "m1a": {(0, 0): first},
        "m1b": {(1, 0): first, (1, 1): second, (0, 1): second},
        "m2": {(0, 2): third, (1, 2): third},
    }
    acc = fisher
    for name, left in calls.items():
        acc = add_product(acc, left, right, scale, place, name == "m2")
    return acc


def solution(mesh):
    return jax.shard_map(
        step,
        mesh=mesh,
        in_specs=(P("row", "col"), P(("row", "col"), None)),
        out_specs=P("row", "col"),
        check_vma=False,
    )
```

time: 259 us -> 175 us (0.68)
  waiting for transfers between devices: 144 us -> 53.3 us
  starting transfers between devices: 0.04 us -> 55.5 us
  matrix products: 45 us -> 0 us
  Pallas kernels: 0 us -> 25.4 us
  blocking collectives: 44.5 us -> 24.9 us
  between operations: 13.4 us -> 0.44 us
  other arithmetic: 0 us -> 3.25 us
    all_gather x2 -> x0, waiting for transfers between devices: 144 us -> none  [the longest x1 106 us: row_panel(): lax.all_gather(pieces.reshape(rows, n_row, 1, t_row), 'col', axis=2, tile...]
    ppermute x0 -> x30, starting transfers between devices: none -> 47.4 us  [send(): return lax.ppermute(value, AXES, pairs)]
    ppermute x0 -> x30, waiting for transfers between devices: none -> 46 us  [send(): return lax.ppermute(value, AXES, pairs)]
    dot_general x1 -> x0, matrix products: 45 us -> none  [transposed_product(): lax.dot_general(left, right, (((0, 1, 2), (0, 1, 2)), ((), ())), precisio...]
    pallas_call x0 -> x5, Pallas kernels: none -> 25.4 us  [the longest x3 21.1 us: add_product(): pl.pallas_call(functools.partial(product_kernel, tuple(parts), len(buffer...]
    all_to_all x2 -> x1, blocking collectives: 44.5 us -> 24.9 us  [exchange(): lax.all_to_all(slab.reshape(rows, n, order // n), axis, split_axis=1, con...]
    all_gather x1 -> x0, local copies, waits for them, and re-layouts: 11.5 us -> none  [direct_product(): lax.all_gather(local_right, 'row', axis=1, tiled=True)]
    unnamed x0 -> x44, local copies, waits for them, and re-layouts: none -> 10.1 us
  transfers between devices with their start and end apart: 2 -> 31, of which waited for: 2 -> 9; matrix products, arithmetic and copies ran while one was open for 4% -> 2% of each run, Pallas kernels for 0% -> 13%
where the time goes in v2:
time: 175 us; the launch traced here: 173 us
  starting transfers between devices  55.5 us (32%)
  waiting for transfers between devices  53.3 us (30%)
  Pallas kernels  25.4 us (15%)
  blocking collectives  24.9 us (14%)
  local copies, waits for them, and re-layouts  10.1 us (6%)
  other arithmetic  3.25 us (2%)
    ppermute x30, starting transfers between devices, send(): return lax.ppermute(value, AXES, pairs)  47.4 us
    ppermute x30, waiting for transfers between devices, send(): return lax.ppermute(value, AXES, pairs)  46 us
    all_to_all x1, blocking collectives, exchange(): lax.all_to_all(slab.reshape(rows, n, order // n), axis, split_axis=1, con...  24.9 us
    pallas_call x3, Pallas kernels, add_product(): pl.pallas_call(functools.partial(product_kernel, tuple(parts), len(buffer...  21.1 us
    unnamed x44, local copies, waits for them, and re-layouts  10.1 us
    all_to_all x1, starting transfers between devices, exchange(): lax.all_to_all(slab.reshape(rows, n, order // n), axis, split_axis=1, con...  8.04 us
    all_to_all x1, waiting for transfers between devices, exchange(): lax.all_to_all(slab.reshape(rows, n, order // n), axis, split_axis=1, con...  7.3 us
    pallas_call x2, Pallas kernels, prepare(): pl.pallas_call(prepare_kernel, out_shape=[jax.ShapeDtypeStruct((k, m), jn...  4.29 us
  transfers between devices with their start and end apart: 31, of which 9 were waited for; matrix products, arithmetic and copies ran while one was open for 2% of the time, Pallas kernels for 13%

profile of v2, /device:TPU:37, one launch (start us, length us, event | category | flops | bytes accessed | tf_op | source)
XLA Modules:
  0.0 172.9 jit_solution(14186361867346468983)
XLA Ops:
  0.0 24.9 %all_to_all.10 = f32[8,16,1024]{2,0,1:T(8,128)S(1)} all-to-all(f32[8,16,1024]{2,0,1:T(8,128)} %bitcast.16), channel_id=1, replica_groups=mesh['row'=16,'col'=16] {'col'}, dimensions={1} | all-to-all | bytes 1048576 | tf_op jit(solution)/shard_map/all_to_all | solution.py:50
  24.9 8.0 %all-to-all-start = ((f32[8,16,1024]{2,0,1:T(8,128)}), f32[8,16,1024]{2,0,1:T(8,128)S(1)}, u32[]{:S(2)}, u32[]{:S(2)}) async-start(f32[8,16,1024]{2,0,1:T(8,128)} %bitcast.17), calls=%async_computation | async-start | bytes 1048576 | tf_op jit(solution)/shard_map/all_to_all | solution.py:50
  32.9 2.4 %collective-permute-start.11 = (f32[16,8,1024]{2,1,0:T(8,128)S(1)}, f32[16,8,1024]{2,1,0:T(8,128)}, u32[]{:S(2)}, u32[]{:S(2)}) collective-permute-start(f32[16,8,1024]{2,1,0:T(8,128)S(1)} %bitcast.11), channel_id=1, source_target_pairs={{64,0},{65,1},{66,2},{67,3},{68,4},{69,5},{70,6},{71,7},{72,8},{73... | collective-permute-start | bytes 1572872 | tf_op jit(solution)/shard_map/ppermute | solution.py:39
  35.4 7.3 %all-to-all-done = f32[8,16,1024]{2,0,1:T(8,128)S(1)} async-done(((f32[8,16,1024]{2,0,1:T(8,128)}), f32[8,16,1024]{2,0,1:T(8,128)S(1)}, u32[]{:S(2)}, u32[]{:S(2)}) %all-to-all-start) | async-done | bytes 524320 | tf_op jit(solution)/shard_map/all_to_all | solution.py:50
  42.6 1.2 collective-permute-start.3
  43.8 1.2 collective-permute-start.4
  45.0 1.0 collective-permute-start.10
  46.0 6.1 %collective-permute-done.11.refs_2_ = f32[16,8,1024]{2,1,0:T(8,128)} collective-permute-done((f32[16,8,1024]{2,1,0:T(8,128)S(1)}, f32[16,8,1024]{2,1,0:T(8,128)}, u32[]{:S(2)}, u32[]{:S(2)}) %collective-permute-start.11) | collective-permute-done | bytes 524320 | tf_op jit(solution)/shard_map/ppermute | solution.py:39
  52.1 0.7 collective-permute-start
  52.8 0.7 collective-permute-done.13.refs_4_
  53.5 1.2 collective-permute-start.1
  54.7 1.1 broadcast_select_fusion.2
  55.8 12.4 %collective-permute-done.3.refs_4_ = f32[16,8,1024]{2,1,0:T(8,128)S(1)} collective-permute-done((f32[16,8,1024]{2,1,0:T(8,128)S(1)}, f32[16,8,1024]{2,1,0:T(8,128)S(1)}, u32[]{:S(2)}, u32[]{:S(2)}) %collective-permute-start.3) | collective-permute-done | bytes 524320 | tf_op jit(solution)/shard_map/ppermute | solution.py:39
  68.2 1.9 %collective-permute-done.4.refs_5_ = f32[16,8,1024]{2,1,0:T(8,128)S(1)} collective-permute-done((f32[16,8,1024]{2,1,0:T(8,128)S(1)}, f32[16,8,1024]{2,1,0:T(8,128)S(1)}, u32[]{:S(2)}, u32[]{:S(2)}) %collective-permute-start.4) | collective-permute-done | bytes 524320 | tf_op jit(solution)/shard_map/ppermute | solution.py:39
  70.2 0.7 collective-permute-start.15
  70.9 0.1 broadcast_select_fusion.3
  71.0 0.0 collective-permute-done.10.refs_1_
  71.0 0.8 copy-done.5
  71.8 0.6 collective-permute-start.12
  72.4 0.0 collective-permute-done.refs_1_
  72.4 0.0 collective-permute-start.14
  72.4 0.0 collective-permute-done.1.refs_2_
  72.4 0.8 collective-permute-start.9
  73.2 13.3 %collective-permute-done.21.refs_0_ = f32[16,8,1024]{2,1,0:T(8,128)} collective-permute-done((f32[16,8,1024]{2,1,0:T(8,128)S(1)}, f32[16,8,1024]{2,1,0:T(8,128)}, u32[]{:S(2)}, u32[]{:S(2)}) %collective-permute-start.21) | collective-permute-done | bytes 524320 | tf_op jit(solution)/shard_map/ppermute | solution.py:39
  86.5 0.5 collective-permute-start.23
  86.9 1.0 collective-permute-start.25
  87.9 0.1 broadcast_select_fusion.4
  88.0 0.0 collective-permute-done.12.refs_3_
  88.0 0.8 copy-done.11
  88.9 1.2 collective-permute-start.2
  90.1 0.8 copy-done.15
  90.9 0.3 collective-permute-start.5
  91.1 1.6 collective-permute-start.8
  92.8 4.1 %collective-permute-done.23.refs_2_ = f32[16,8,1024]{2,1,0:T(8,128)S(1)} collective-permute-done((f32[16,8,1024]{2,1,0:T(8,128)}, f32[16,8,1024]{2,1,0:T(8,128)S(1)}, u32[]{:S(2)}, u32[]{:S(2)}) %collective-permute-start.23) | collective-permute-done | bytes 524320 | tf_op jit(solution)/shard_map/ppermute | solution.py:39
  96.9 1.2 collective-permute-start.6
  98.1 0.9 collective-permute-done.25.refs_4_
  99.0 0.9 collective-permute-start.7
  99.9 0.9 broadcast_select_fusion.1
  100.8 0.8 copy-done.7
  101.6 6.7 %collective-permute-start.22 = (f32[16,8,1024]{2,1,0:T(8,128)}, f32[16,8,1024]{2,1,0:T(8,128)}, u32[]{:S(2)}, u32[]{:S(2)}) collective-permute-start(f32[16,8,1024]{2,1,0:T(8,128)} %collective-permute-done.21.refs_0_), channel_id=1, source_target_pairs={{16,0},{17,1},{18,2},{19,3},{20,4},{21,5},{22,6},{23,7},{24,8},{25... | collective-permute-start | bytes 1572872 | tf_op jit(solution)/shard_map/ppermute | solution.py:39
  108.3 8.6 %collective-permute-start.16 = (f32[16,8,1024]{2,1,0:T(8,128)}, f32[16,8,1024]{2,1,0:T(8,128)}, u32[]{:S(2)}, u32[]{:S(2)}) collective-permute-start(f32[16,8,1024]{2,1,0:T(8,128)} %collective-permute-done.15.refs_6_), channel_id=1, source_target_pairs={{16,0},{17,1},{18,2},{19,3},{20,4},{21,5},{22,6},{23,7},{24,8},{25... | collective-permute-start | bytes 1572872 | tf_op jit(solution)/shard_map/ppermute | solution.py:39
  116.9 1.3 collective-permute-start.27
  118.2 0.8 copy-done.17
  118.9 0.7 collective-permute-start.19
  119.7 0.8 copy-done.20
  120.5 2.0 %collective-permute-start.20 = (f32[16,8,1024]{2,1,0:T(8,128)}, f32[16,8,1024]{2,1,0:T(8,128)}, u32[]{:S(2)}, u32[]{:S(2)}) collective-permute-start(f32[16,8,1024]{2,1,0:T(8,128)} %collective-permute-done.9.refs_10_), channel_id=1, source_target_pairs={{12,0},{13,1},{14,2},{15,3},{0,4},{1,5},{2,6},{3,7},{4,8},{5,9},{6... | collective-permute-start | bytes 1572872 | tf_op jit(solution)/shard_map/ppermute | solution.py:39
  122.5 0.1 pad_add_fusion.place
  122.6 3.8 %collective-permute-start.24 = (f32[16,8,1024]{2,1,0:T(8,128)}, f32[16,8,1024]{2,1,0:T(8,128)S(1)}, u32[]{:S(2)}, u32[]{:S(2)}) collective-permute-start(f32[16,8,1024]{2,1,0:T(8,128)} %copy-done.1), channel_id=1, source_target_pairs={{16,0},{17,1},{18,2},{19,3},{20,4},{21,5},{22,6},{23,7},{24,8},{25... | collective-permute-start | bytes 1572872 | tf_op jit(solution)/shard_map/ppermute | solution.py:39
  126.4 0.1 collective-permute-start.26
  126.5 6.5 %collective-permute-done.19.refs_13_ = f32[16,8,1024]{2,1,0:T(8,128)} collective-permute-done((f32[16,8,1024]{2,1,0:T(8,128)}, f32[16,8,1024]{2,1,0:T(8,128)}, u32[]{:S(2)}, u32[]{:S(2)}) %collective-permute-start.19) | collective-permute-done | bytes 524320 | tf_op jit(solution)/shard_map/ppermute | solution.py:39
  133.0 2.4 %collective-permute-start.18 = (f32[16,8,1024]{2,1,0:T(8,128)}, f32[16,8,1024]{2,1,0:T(8,128)S(1)}, u32[]{:S(2)}, u32[]{:S(2)}) collective-permute-start(f32[16,8,1024]{2,1,0:T(8,128)} %copy-done.13), channel_id=1, source_target_pairs={{12,0},{13,1},{14,2},{15,3},{0,4},{1,5},{2,6},{3,7},{4,8},{5,9},{6... | collective-permute-start | bytes 1572872 | tf_op jit(solution)/shard_map/ppermute | solution.py:39
  135.4 4.0 %collective-permute-start.28 = (f32[16,8,1024]{2,1,0:T(8,128)}, f32[16,8,1024]{2,1,0:T(8,128)S(1)}, u32[]{:S(2)}, u32[]{:S(2)}) collective-permute-start(f32[16,8,1024]{2,1,0:T(8,128)} %collective-permute-done.27.refs_6_), channel_id=1, source_target_pairs={{16,0},{17,1},{18,2},{19,3},{20,4},{21,5},{22,6},{23,7},{24,8},{25... | collective-permute-start | bytes 1572872 | tf_op jit(solution)/shard_map/ppermute | solution.py:39
  139.4 1.1 broadcast_select_fusion
  140.5 1.0 copy-done.6
  141.6 1.0 copy-done.12
  142.6 1.0 copy-done.16
  143.7 2.3 %shard_map.28 = (bf16[704,1024]{1,0:T(8,128)(2,1)S(1)}, bf16[704,1024]{1,0:T(8,128)(2,1)S(1)}, bf16[256,1024]{1,0:T(8,128)(2,1)S(1)}, bf16[256,1024]{1,0:T(8,128...) custom-call(s32[2]{0:T(128)S(1)} %pad_add_fusion.place, f32[16,8,1024]{2,1,0:T(8,128)S(1)} %bitcast.15, ...), custom_call_target="tpu_custom_call" | custom-call | flops 4194304 | bytes 8388608 | tf_op jit(solution)/shard_map/pallas_call | solution.py:80
  146.0 1.0 copy-done.18
  147.0 1.0 copy-done.21
  148.1 6.9 %shard_map.29.acc = f32[1024,1024]{1,0:T(8,128)S(1)} custom-call(s32[2]{0:T(128)S(1)} %pad_add_fusion.place, f32[1024,1024]{1,0:T(8,128)S(1)} %copy-done, f32[16,8,1024]{2,1,0:T(8,128)S(1)} %bitcast.9, f32[16,8,1024]{2,1,0:T(8,128)S(1)} %collective-permute-done.refs_1_, f32[16,8,1024]{2,1,0:T(8,128)S(1)} %collective-permute-done.1.refs_2_, ...), custom_call_target="tpu_custom_call" | custom-call | flops 4429185024 | bytes 14155776 | tf_op jit(solution)/shard_map/pallas_call | solution.py:172
  155.1 1.4 collective-permute-start.29
  156.5 2.0 %shard_map.30 = (bf16[704,1024]{1,0:T(8,128)(2,1)S(1)}, bf16[704,1024]{1,0:T(8,128)(2,1)S(1)}, bf16[256,1024]{1,0:T(8,128)(2,1)S(1)}, bf16[256,1024]{1,0:T(8,128...) custom-call(s32[2]{0:T(128)S(1)} %pad_add_fusion.place, ...), custom_call_target="tpu_custom_call" | custom-call | flops 4194304 | bytes 8388608 | tf_op jit(solution)/shard_map/pallas_call | solution.py:80
  158.6 10.8 %shard_map.31.acc = f32[1024,1024]{1,0:T(8,128)S(1)} custom-call(s32[2]{0:T(128)S(1)} %pad_add_fusion.place, f32[1024,1024]{1,0:T(8,128)S(1)} %shard_map.29.acc, f32[16,8,1024]{2,1,0:T(8,128)S(1)} %bitcast.10, f32[16,8,1024]{2,1,0:T(8,128)S(1)} %collective-permute-done.refs_1_, f32[16,8,1024]{2,1,0:T(8,128)S(1)} %collective-permute-done.1.refs_2_, ...), custom_call_target="tpu_custom_call" | custom-call | flops 7650410496 | bytes 18350080 | tf_op jit(solution)/shard_map/pallas_call | solution.py:172
  169.3 3.4 %shard_map.32 = f32[1024,1024]{1,0:T(8,128)} custom-call(s32[2]{0:T(128)S(1)} %pad_add_fusion.place, f32[1024,1024]{1,0:T(8,128)S(1)} %shard_map.31.acc, f32[16,8,1024]{2,1,0:T(8,128)S(1)} %collective-permute-done.29.refs_0_, bf16[64,1024]{1,0:T(8,128)(2,1)S(1)} %get-tuple-element.25.refs_1_, bf16[64,1024]{1,0:T(8,128)(2,1)S(1)} %get-tuple-element.26.refs_2_, ...), custom_call_target="tpu_custom_call" | custom-call | flops 805306368 | bytes 9437184 | tf_op jit(solution)/shard_map/pallas_call | solution.py:172
  (54 shorter events, 0.1 us)
Async XLA Ops:
  24.9 17.7 %all-to-all-start = ((f32[8,16,1024]{2,0,1:T(8,128)}), f32[8,16,1024]{2,0,1:T(8,128)S(1)}, u32[]{:S(2)}, u32[]{:S(2)}) async-start(f32[8,16,1024]{2,0,1:T(8,128)} %bitcast.17), calls=%async_computation | async-start | bytes 1048576 | tf_op jit(solution)/shard_map/all_to_all | solution.py:50
  32.9 19.1 %collective-permute-start.11 = (f32[16,8,1024]{2,1,0:T(8,128)S(1)}, f32[16,8,1024]{2,1,0:T(8,128)}, u32[]{:S(2)}, u32[]{:S(2)}) collective-permute-start(f32[16,8,1024]{2,1,0:T(8,128)S(1)} %bitcast.11), channel_id=1, source_target_pairs={{64,0},{65,1},{66,2},{67,3},{68,4},{69,5},{70,6},{71,7},{72,8},{73... | collective-permute-start | bytes 1572872 | tf_op jit(solution)/shard_map/ppermute | solution.py:39
  35.3 18.2 %collective-permute-start.13 = (f32[16,8,1024]{2,1,0:T(8,128)S(1)}, f32[16,8,1024]{2,1,0:T(8,128)}, u32[]{:S(2)}, u32[]{:S(2)}) collective-permute-start(f32[16,8,1024]{2,1,0:T(8,128)S(1)} %bitcast.12), channel_id=1, source_target_pairs={{192,0},{193,1},{194,2},{195,3},{196,4},{197,5},{198,6},{199,7},{2... | collective-permute-start | bytes 1572872 | tf_op jit(solution)/shard_map/ppermute | solution.py:39
  42.6 25.6 %collective-permute-start.3 = (f32[16,8,1024]{2,1,0:T(8,128)S(1)}, f32[16,8,1024]{2,1,0:T(8,128)S(1)}, u32[]{:S(2)}, u32[]{:S(2)}) collective-permute-start(f32[16,8,1024]{2,1,0:T(8,128)S(1)} %bitcast.5), channel_id=1, source_target_pairs={{1,0},{2,1},{3,2},{0,3},{5,4},{6,5},{7,6},{4,7},{9,8},{10,9},{11,1... | collective-permute-start | bytes 1572872 | tf_op jit(solution)/shard_map/ppermute | solution.py:39
  43.8 26.3 %collective-permute-start.4 = (f32[16,8,1024]{2,1,0:T(8,128)S(1)}, f32[16,8,1024]{2,1,0:T(8,128)S(1)}, u32[]{:S(2)}, u32[]{:S(2)}) collective-permute-start(f32[16,8,1024]{2,1,0:T(8,128)S(1)} %bitcast.6), channel_id=1, source_target_pairs={{3,0},{0,1},{1,2},{2,3},{7,4},{4,5},{5,6},{6,7},{11,8},{8,9},{9,10... | collective-permute-start | bytes 1572872 | tf_op jit(solution)/shard_map/ppermute | solution.py:39
  45.0 26.0 %collective-permute-start.10 = (f32[16,8,1024]{2,1,0:T(8,128)S(1)}, f32[16,8,1024]{2,1,0:T(8,128)S(1)}, u32[]{:S(2)}, u32[]{:S(2)}) collective-permute-start(f32[16,8,1024]{2,1,0:T(8,128)S(1)} %bitcast.13), channel_id=1, source_target_pairs={{16,0},{17,1},{18,2},{19,3},{20,4},{21,5},{22,6},{23,7},{24,8},{25... | collective-permute-start | bytes 1572872 | tf_op jit(solution)/shard_map/ppermute | solution.py:39
  52.1 20.3 %collective-permute-start = (f32[16,8,1024]{2,1,0:T(8,128)S(1)}, f32[16,8,1024]{2,1,0:T(8,128)S(1)}, u32[]{:S(2)}, u32[]{:S(2)}) collective-permute-start(f32[16,8,1024]{2,1,0:T(8,128)S(1)} %bitcast.7), channel_id=1, source_target_pairs={{4,0},{5,1},{6,2},{7,3},{8,4},{9,5},{10,6},{11,7},{12,8},{13,9},{1... | collective-permute-start | bytes 1572872 | tf_op jit(solution)/shard_map/ppermute | solution.py:39
  53.5 18.9 %collective-permute-start.1 = (f32[16,8,1024]{2,1,0:T(8,128)S(1)}, f32[16,8,1024]{2,1,0:T(8,128)S(1)}, u32[]{:S(2)}, u32[]{:S(2)}) collective-permute-start(f32[16,8,1024]{2,1,0:T(8,128)S(1)} %bitcast.8), channel_id=1, source_target_pairs={{12,0},{13,1},{14,2},{15,3},{0,4},{1,5},{2,6},{3,7},{4,8},{5,9},{6... | collective-permute-start | bytes 1572872 | tf_op jit(solution)/shard_map/ppermute | solution.py:39
  68.2 18.2 %collective-permute-start.21 = (f32[16,8,1024]{2,1,0:T(8,128)S(1)}, f32[16,8,1024]{2,1,0:T(8,128)}, u32[]{:S(2)}, u32[]{:S(2)}) collective-permute-start(f32[16,8,1024]{2,1,0:T(8,128)S(1)} %bitcast.14), channel_id=1, source_target_pairs={{32,0},{33,1},{34,2},{35,3},{36,4},{37,5},{38,6},{39,7},{40,8},{41... | collective-permute-start | bytes 1572872 | tf_op jit(solution)/shard_map/ppermute | solution.py:39
  70.2 16.8 %collective-permute-start.15 = (f32[16,8,1024]{2,1,0:T(8,128)S(1)}, f32[16,8,1024]{2,1,0:T(8,128)}, u32[]{:S(2)}, u32[]{:S(2)}) collective-permute-start(f32[16,8,1024]{2,1,0:T(8,128)S(1)} %broadcast_select_fusion.2), channel_id=1, source_target_pairs={{64,0},{65,1},{66,2},{67,3},{68,4},{69,5},{70,6},{71,7},{72,8},{73... | collective-permute-start | bytes 1572872 | tf_op jit(solution)/shard_map/ppermute | solution.py:39
  71.0 0.8 copy-start.5
  71.8 16.2 %collective-permute-start.12 = (f32[16,8,1024]{2,1,0:T(8,128)}, f32[16,8,1024]{2,1,0:T(8,128)S(1)}, u32[]{:S(2)}, u32[]{:S(2)}) collective-permute-start(f32[16,8,1024]{2,1,0:T(8,128)} %collective-permute-done.11.refs_2_), channel_id=1, source_target_pairs={{16,0},{17,1},{18,2},{19,3},{20,4},{21,5},{22,6},{23,7},{24,8},{25... | collective-permute-start | bytes 1572872 | tf_op jit(solution)/shard_map/ppermute | solution.py:39
  72.4 17.6 %collective-permute-start.14 = (f32[16,8,1024]{2,1,0:T(8,128)}, f32[16,8,1024]{2,1,0:T(8,128)S(1)}, u32[]{:S(2)}, u32[]{:S(2)}) collective-permute-start(f32[16,8,1024]{2,1,0:T(8,128)} %collective-permute-done.13.refs_4_), channel_id=1, source_target_pairs={{16,0},{17,1},{18,2},{19,3},{20,4},{21,5},{22,6},{23,7},{24,8},{25... | collective-permute-start | bytes 1572872 | tf_op jit(solution)/shard_map/ppermute | solution.py:39
  72.4 18.7 %collective-permute-start.9 = (f32[16,8,1024]{2,1,0:T(8,128)S(1)}, f32[16,8,1024]{2,1,0:T(8,128)}, u32[]{:S(2)}, u32[]{:S(2)}) collective-permute-start(f32[16,8,1024]{2,1,0:T(8,128)S(1)} %broadcast_select_fusion.3), channel_id=1, source_target_pairs={{1,0},{2,1},{3,2},{0,3},{5,4},{6,5},{7,6},{4,7},{9,8},{10,9},{11,1... | collective-permute-start | bytes 1572872 | tf_op jit(solution)/shard_map/ppermute | solution.py:39
  86.5 10.4 %collective-permute-start.23 = (f32[16,8,1024]{2,1,0:T(8,128)}, f32[16,8,1024]{2,1,0:T(8,128)S(1)}, u32[]{:S(2)}, u32[]{:S(2)}) collective-permute-start(f32[16,8,1024]{2,1,0:T(8,128)} %collective-permute-done.21.refs_0_), channel_id=1, source_target_pairs={{64,0},{65,1},{66,2},{67,3},{68,4},{69,5},{70,6},{71,7},{72,8},{73... | collective-permute-start | bytes 1572872 | tf_op jit(solution)/shard_map/ppermute | solution.py:39
  86.9 12.1 %collective-permute-start.25 = (f32[16,8,1024]{2,1,0:T(8,128)}, f32[16,8,1024]{2,1,0:T(8,128)S(1)}, u32[]{:S(2)}, u32[]{:S(2)}) collective-permute-start(f32[16,8,1024]{2,1,0:T(8,128)} %collective-permute-done.21.refs_0_), channel_id=1, source_target_pairs={{192,0},{193,1},{194,2},{195,3},{196,4},{197,5},{198,6},{199,7},{2... | collective-permute-start | bytes 1572872 | tf_op jit(solution)/shard_map/ppermute | solution.py:39
  88.0 0.9 copy-start.11
  88.9 11.9 %collective-permute-start.2 = (f32[16,8,1024]{2,1,0:T(8,128)S(1)}, f32[16,8,1024]{2,1,0:T(8,128)S(1)}, u32[]{:S(2)}, u32[]{:S(2)}) collective-permute-start(f32[16,8,1024]{2,1,0:T(8,128)S(1)} %broadcast_select_fusion.4), channel_id=1, source_target_pairs={{4,0},{5,1},{6,2},{7,3},{8,4},{9,5},{10,6},{11,7},{12,8},{13,9},{1... | collective-permute-start | bytes 1572872 | tf_op jit(solution)/shard_map/ppermute | solution.py:39
  90.1 0.8 copy-start.15
  90.9 17.4 %collective-permute-start.5 = (f32[16,8,1024]{2,1,0:T(8,128)S(1)}, f32[16,8,1024]{2,1,0:T(8,128)S(1)}, u32[]{:S(2)}, u32[]{:S(2)}) collective-permute-start(f32[16,8,1024]{2,1,0:T(8,128)S(1)} %collective-permute-done.3.refs_4_), channel_id=1, source_target_pairs={{4,0},{5,1},{6,2},{7,3},{8,4},{9,5},{10,6},{11,7},{12,8},{13,9},{1... | collective-permute-start | bytes 1572872 | tf_op jit(solution)/shard_map/ppermute | solution.py:39
  91.1 25.8 %collective-permute-start.8 = (f32[16,8,1024]{2,1,0:T(8,128)S(1)}, f32[16,8,1024]{2,1,0:T(8,128)S(1)}, u32[]{:S(2)}, u32[]{:S(2)}) collective-permute-start(f32[16,8,1024]{2,1,0:T(8,128)S(1)} %collective-permute-done.4.refs_5_), channel_id=1, source_target_pairs={{12,0},{13,1},{14,2},{15,3},{0,4},{1,5},{2,6},{3,7},{4,8},{5,9},{6... | collective-permute-start | bytes 1572872 | tf_op jit(solution)/shard_map/ppermute | solution.py:39
  96.9 22.8 %copy-start.1 = (f32[16,8,1024]{2,1,0:T(8,128)}, f32[16,8,1024]{2,1,0:T(8,128)S(1)}, u32[]{:S(2)}) copy-start(f32[16,8,1024]{2,1,0:T(8,128)S(1)} %collective-permute-done.23.refs_2_) | copy-start | bytes 1572868
  96.9 21.2 %collective-permute-start.6 = (f32[16,8,1024]{2,1,0:T(8,128)S(1)}, f32[16,8,1024]{2,1,0:T(8,128)S(1)}, u32[]{:S(2)}, u32[]{:S(2)}) collective-permute-start(f32[16,8,1024]{2,1,0:T(8,128)S(1)} %collective-permute-done.3.refs_4_), channel_id=1, source_target_pairs={{12,0},{13,1},{14,2},{15,3},{0,4},{1,5},{2,6},{3,7},{4,8},{5,9},{6... | collective-permute-start | bytes 1572872 | tf_op jit(solution)/shard_map/ppermute | solution.py:39
  99.0 20.6 %copy-start.3 = (f32[16,8,1024]{2,1,0:T(8,128)}, f32[16,8,1024]{2,1,0:T(8,128)S(1)}, u32[]{:S(2)}) copy-start(f32[16,8,1024]{2,1,0:T(8,128)S(1)} %collective-permute-done.25.refs_4_) | copy-start | bytes 1572868
  99.0 20.6 %collective-permute-start.7 = (f32[16,8,1024]{2,1,0:T(8,128)S(1)}, f32[16,8,1024]{2,1,0:T(8,128)S(1)}, u32[]{:S(2)}, u32[]{:S(2)}) collective-permute-start(f32[16,8,1024]{2,1,0:T(8,128)S(1)} %collective-permute-done.4.refs_5_), channel_id=1, source_target_pairs={{4,0},{5,1},{6,2},{7,3},{8,4},{9,5},{10,6},{11,7},{12,8},{13,9},{1... | collective-permute-start | bytes 1572872 | tf_op jit(solution)/shard_map/ppermute | solution.py:39
  100.8 0.8 copy-start.7
  101.6 21.0 %collective-permute-start.22 = (f32[16,8,1024]{2,1,0:T(8,128)}, f32[16,8,1024]{2,1,0:T(8,128)}, u32[]{:S(2)}, u32[]{:S(2)}) collective-permute-start(f32[16,8,1024]{2,1,0:T(8,128)} %collective-permute-done.21.refs_0_), channel_id=1, source_target_pairs={{16,0},{17,1},{18,2},{19,3},{20,4},{21,5},{22,6},{23,7},{24,8},{25... | collective-permute-start | bytes 1572872 | tf_op jit(solution)/shard_map/ppermute | solution.py:39
  108.3 11.4 %copy-start.9 = (f32[16,8,1024]{2,1,0:T(8,128)}, f32[16,8,1024]{2,1,0:T(8,128)S(1)}, u32[]{:S(2)}) copy-start(f32[16,8,1024]{2,1,0:T(8,128)S(1)} %collective-permute-done.5.refs_6_) | copy-start | bytes 1572868
  108.3 18.1 %collective-permute-start.16 = (f32[16,8,1024]{2,1,0:T(8,128)}, f32[16,8,1024]{2,1,0:T(8,128)}, u32[]{:S(2)}, u32[]{:S(2)}) collective-permute-start(f32[16,8,1024]{2,1,0:T(8,128)} %collective-permute-done.15.refs_6_), channel_id=1, source_target_pairs={{16,0},{17,1},{18,2},{19,3},{20,4},{21,5},{22,6},{23,7},{24,8},{25... | collective-permute-start | bytes 1572872 | tf_op jit(solution)/shard_map/ppermute | solution.py:39
  116.9 2.8 %copy-start.13 = (f32[16,8,1024]{2,1,0:T(8,128)}, f32[16,8,1024]{2,1,0:T(8,128)S(1)}, u32[]{:S(2)}) copy-start(f32[16,8,1024]{2,1,0:T(8,128)S(1)} %collective-permute-done.8.refs_9_) | copy-start | bytes 1572868
  116.9 9.6 %collective-permute-start.27 = (f32[16,8,1024]{2,1,0:T(8,128)}, f32[16,8,1024]{2,1,0:T(8,128)}, u32[]{:S(2)}, u32[]{:S(2)}) collective-permute-start(f32[16,8,1024]{2,1,0:T(8,128)} %broadcast_select_fusion.1), channel_id=1, source_target_pairs={{64,0},{65,1},{66,2},{67,3},{68,4},{69,5},{70,6},{71,7},{72,8},{73... | collective-permute-start | bytes 1572872 | tf_op jit(solution)/shard_map/ppermute | solution.py:39
  118.1 0.8 copy-start.17
  118.9 14.1 %collective-permute-start.19 = (f32[16,8,1024]{2,1,0:T(8,128)}, f32[16,8,1024]{2,1,0:T(8,128)}, u32[]{:S(2)}, u32[]{:S(2)}) collective-permute-start(f32[16,8,1024]{2,1,0:T(8,128)} %collective-permute-done.9.refs_10_), channel_id=1, source_target_pairs={{4,0},{5,1},{6,2},{7,3},{8,4},{9,5},{10,6},{11,7},{12,8},{13,9},{1... | collective-permute-start | bytes 1572872 | tf_op jit(solution)/shard_map/ppermute | solution.py:39
  119.7 0.8 copy-start.20
  120.5 14.9 %collective-permute-start.20 = (f32[16,8,1024]{2,1,0:T(8,128)}, f32[16,8,1024]{2,1,0:T(8,128)}, u32[]{:S(2)}, u32[]{:S(2)}) collective-permute-start(f32[16,8,1024]{2,1,0:T(8,128)} %collective-permute-done.9.refs_10_), channel_id=1, source_target_pairs={{12,0},{13,1},{14,2},{15,3},{0,4},{1,5},{2,6},{3,7},{4,8},{5,9},{6... | collective-permute-start | bytes 1572872 | tf_op jit(solution)/shard_map/ppermute | solution.py:39
  122.5 23.5 %copy-start = (f32[1024,1024]{1,0:T(8,128)S(1)}, f32[1024,1024]{1,0:T(8,128)}, u32[]{:S(2)}) copy-start(f32[1024,1024]{1,0:T(8,128)} %acc.1) | copy-start | bytes 12582916
  122.6 32.5 %collective-permute-start.24 = (f32[16,8,1024]{2,1,0:T(8,128)}, f32[16,8,1024]{2,1,0:T(8,128)S(1)}, u32[]{:S(2)}, u32[]{:S(2)}) collective-permute-start(f32[16,8,1024]{2,1,0:T(8,128)} %copy-done.1), channel_id=1, source_target_pairs={{16,0},{17,1},{18,2},{19,3},{20,4},{21,5},{22,6},{23,7},{24,8},{25... | collective-permute-start | bytes 1572872 | tf_op jit(solution)/shard_map/ppermute | solution.py:39
  126.4 30.1 %collective-permute-start.26 = (f32[16,8,1024]{2,1,0:T(8,128)}, f32[16,8,1024]{2,1,0:T(8,128)S(1)}, u32[]{:S(2)}, u32[]{:S(2)}) collective-permute-start(f32[16,8,1024]{2,1,0:T(8,128)} %copy-done.3), channel_id=1, source_target_pairs={{16,0},{17,1},{18,2},{19,3},{20,4},{21,5},{22,6},{23,7},{24,8},{25... | collective-permute-start | bytes 1572872 | tf_op jit(solution)/shard_map/ppermute | solution.py:39
  126.5 32.0 %collective-permute-start.17 = (f32[16,8,1024]{2,1,0:T(8,128)}, f32[16,8,1024]{2,1,0:T(8,128)S(1)}, u32[]{:S(2)}, u32[]{:S(2)}) collective-permute-start(f32[16,8,1024]{2,1,0:T(8,128)} %copy-done.9), channel_id=1, source_target_pairs={{4,0},{5,1},{6,2},{7,3},{8,4},{9,5},{10,6},{11,7},{12,8},{13,9},{1... | collective-permute-start | bytes 1572872 | tf_op jit(solution)/shard_map/ppermute | solution.py:39
  133.0 25.5 %collective-permute-start.18 = (f32[16,8,1024]{2,1,0:T(8,128)}, f32[16,8,1024]{2,1,0:T(8,128)S(1)}, u32[]{:S(2)}, u32[]{:S(2)}) collective-permute-start(f32[16,8,1024]{2,1,0:T(8,128)} %copy-done.13), channel_id=1, source_target_pairs={{12,0},{13,1},{14,2},{15,3},{0,4},{1,5},{2,6},{3,7},{4,8},{5,9},{6... | collective-permute-start | bytes 1572872 | tf_op jit(solution)/shard_map/ppermute | solution.py:39
  135.4 21.1 %collective-permute-start.28 = (f32[16,8,1024]{2,1,0:T(8,128)}, f32[16,8,1024]{2,1,0:T(8,128)S(1)}, u32[]{:S(2)}, u32[]{:S(2)}) collective-permute-start(f32[16,8,1024]{2,1,0:T(8,128)} %collective-permute-done.27.refs_6_), channel_id=1, source_target_pairs={{16,0},{17,1},{18,2},{19,3},{20,4},{21,5},{22,6},{23,7},{24,8},{25... | collective-permute-start | bytes 1572872 | tf_op jit(solution)/shard_map/ppermute | solution.py:39
  140.5 1.0 copy-start.6
  141.6 1.0 copy-start.12
  142.6 1.0 copy-start.16
  143.7 2.3 %copy-start.8 = (f32[16,8,1024]{2,1,0:T(8,128)S(1)}, f32[16,8,1024]{2,1,0:T(8,128)}, u32[]{:S(2)}) copy-start(f32[16,8,1024]{2,1,0:T(8,128)} %copy-done.7) | copy-start | bytes 1572868
  143.7 2.3 %copy-start.10 = (f32[16,8,1024]{2,1,0:T(8,128)S(1)}, f32[16,8,1024]{2,1,0:T(8,128)}, u32[]{:S(2)}) copy-start(f32[16,8,1024]{2,1,0:T(8,128)} %copy-done.9) | copy-start | bytes 1572868
  143.7 2.3 %copy-start.14 = (f32[16,8,1024]{2,1,0:T(8,128)S(1)}, f32[16,8,1024]{2,1,0:T(8,128)}, u32[]{:S(2)}) copy-start(f32[16,8,1024]{2,1,0:T(8,128)} %copy-done.13) | copy-start | bytes 1572868
  146.0 1.0 copy-start.18
  147.0 1.0 copy-start.21
  148.1 8.4 %copy-start.2 = (f32[16,8,1024]{2,1,0:T(8,128)S(1)}, f32[16,8,1024]{2,1,0:T(8,128)}, u32[]{:S(2)}) copy-start(f32[16,8,1024]{2,1,0:T(8,128)} %copy-done.1) | copy-start | bytes 1572868
  148.1 8.4 %copy-start.4 = (f32[16,8,1024]{2,1,0:T(8,128)S(1)}, f32[16,8,1024]{2,1,0:T(8,128)}, u32[]{:S(2)}) copy-start(f32[16,8,1024]{2,1,0:T(8,128)} %copy-done.3) | copy-start | bytes 1572868
  155.0 3.5 %copy-start.19 = (f32[16,8,1024]{2,1,0:T(8,128)S(1)}, f32[16,8,1024]{2,1,0:T(8,128)}, u32[]{:S(2)}) copy-start(f32[16,8,1024]{2,1,0:T(8,128)} %copy-done.17) | copy-start | bytes 1572868
  155.1 14.3 %collective-permute-start.29 = (f32[16,8,1024]{2,1,0:T(8,128)S(1)}, f32[16,8,1024]{2,1,0:T(8,128)S(1)}, u32[]{:S(2)}, u32[]{:S(2)}) collective-permute-start(f32[16,8,1024]{2,1,0:T(8,128)S(1)} %broadcast_select_fusion), channel_id=1, source_target_pairs={{4,0},{5,1},{6,2},{7,3},{8,4},{9,5},{10,6},{11,7},{12,8},{13,9},{1... | collective-permute-start | bytes 1572872 | tf_op jit(solution)/shard_map/ppermute | solution.py:39

commit v3 on v2

--- a/solution.py
+++ b/solution.py
@@ -10,7 +10,7 @@
 
 AXES = ("row", "col")
 TILE_N = 512
-VMEM_BYTES = 24 << 20
+VMEM_BYTES = 14 << 20
 INSIDE = pl.BlockSpec(memory_space=pltpu.VMEM)
 
 SOURCES = (
@@ -44,11 +44,29 @@
     return send(value, **{axis: (1, -1)})
 
 
-def exchange(slab, axis):
+def row_exchange(slab):
     rows, order = slab.shape
-    n = lax.axis_size(axis)
-    got = lax.all_to_all(slab.reshape(rows, n, order // n), axis, split_axis=1, concat_axis=1, tiled=True)
+    n = lax.axis_size("row")
+    got = lax.all_to_all(slab.reshape(rows, n, order // n), "row", split_axis=1, concat_axis=1, tiled=True)
     return got.transpose(1, 0, 2)
+
+
+def col_exchange(slab):
+    rows, order = slab.shape
+    c = lax.axis_index("col")
+    x, zh = c >> 2, c & 3
+    tile = order // 16
+    held = []
+    for dx in STEPS:
+        piece = lax.dynamic_slice_in_dim(slab, ((x - dx) & 3) * (4 * tile), 4 * tile, axis=1)
+        piece = piece.reshape(rows, 4, tile).transpose(1, 0, 2)
+        held.append(send(piece, dx=dx) if dx else piece)
+    held = jnp.stack(held)
+    got = []
+    for dzh in STEPS:
+        piece = lax.dynamic_slice_in_dim(held, (zh - dzh) & 3, 1, axis=1)[:, 0]
+        got.append(send(piece, dzh=dzh) if dzh else piece)
+    return jnp.concatenate(got, axis=0)
 
 
 def split(value):
@@ -56,9 +74,8 @@
     return high, (value - high.astype(jnp.float32)).astype(jnp.bfloat16)
 
 
-def prepare_kernel(place, *refs):
+def prepare_kernel(*refs):
     pieces, outs = refs[:8], refs[8:]
-    c = place[1]
     width = 256
 
     @pl.loop(0, pieces[0].shape[2] // width)
@@ -67,24 +84,24 @@
         for group, sources in enumerate(SOURCES):
             high, low = outs[2 * group : 2 * group + 2]
             for b, (dx, dzh) in enumerate(sources):
-                at = (((c >> 2) + dx) & 3) * 4 + (((c & 3) + dzh) & 3)
+                at = STEPS.index(dzh) * 4 + STEPS.index(dx)
                 for i in range(4):
                     rows = pl.ds(b * 64 + i * 16, 16)
                     both = jnp.concatenate([pieces[2 * i][at, :, cols], pieces[2 * i + 1][at, :, cols]], axis=0)
                     high[rows, cols], low[rows, cols] = split(both)
 
 
-def prepare(pieces, place):
+def prepare(pieces):
     m = pieces[0].shape[2]
     ks = [64 * len(sources) for sources in SOURCES for _ in range(2)]
     return pl.pallas_call(
         prepare_kernel,
         out_shape=[jax.ShapeDtypeStruct((k, m), jnp.bfloat16) for k in ks],
-        in_specs=[pl.BlockSpec(memory_space=pltpu.SMEM)] + [INSIDE] * len(pieces),
+        in_specs=[INSIDE] * len(pieces),
         out_specs=[INSIDE] * len(ks),
         cost_estimate=pl.CostEstimate(flops=2 * sum(ks) * m, bytes_accessed=4 * sum(ks) * m, transcendentals=0),
         compiler_params=pltpu.CompilerParams(vmem_limit_bytes=VMEM_BYTES),
-    )(place, *pieces)
+    )(*pieces)
 
 
 def product_kernel(parts, n_left, scale, last, place, acc, *refs):
@@ -182,10 +199,10 @@
 
 def step(fisher, slab):
     scale = 1.0 / (slab.shape[0] * lax.axis_size("row") * lax.axis_size("col"))
-    place = jnp.stack([lax.axis_index("row"), lax.axis_index("col")])
-
-    s = exchange(slab, "row")
-    d = exchange(slab, "col")
+    place = lax.axis_index("row")[None]
+
+    s = row_exchange(slab)
+    d = col_exchange(slab)
     zp, zm = send(s, dzh=1), send(s, dzh=-1)
     xp, xm = send(s, dx=1), send(s, dx=-1)
     x2 = relay(xp, xm, "dx")
@@ -205,14 +222,15 @@
         pieces = []
         for value in own:
             pieces += [value, send(value, dk=1)]
-        right[half] = prepare(pieces, place)
+        right[half] = prepare(pieces)
 
     first = [s, xp, xm, x2, zp, zm, bpp, bmp, bpm, bmm, z2]
     second = [b2p, b2m, cp, cm]
     third = [c2]
     calls = {
         "m1a": {(0, 0): first},
-        "m1b": {(1, 0): first, (1, 1): second, (0, 1): second},
+        "m1c": {(0, 1): second},
+        "m1b": {(1, 0): first, (1, 1): second},
         "m2": {(0, 2): third, (1, 2): third},
     }
     acc = fisher

time: 175 us -> 170 us (0.971)
  the two profiles are of different devices: /device:TPU:37 before, /device:TPU:24 now
where the time goes in v3:
time: 170 us
  waiting for transfers between devices  87 us (51%)
  starting transfers between devices  56.3 us (33%)
  Pallas kernels  22.2 us (13%)
  local copies, waits for them, and re-layouts  2.79 us (2%)
    ppermute x36, waiting for transfers between devices, send(): return lax.ppermute(value, AXES, pairs)  87 us
    ppermute x36, starting transfers between devices, send(): return lax.ppermute(value, AXES, pairs)  51.8 us
    pallas_call x4, Pallas kernels, add_product(): pl.pallas_call(functools.partial(product_kernel, tuple(parts), len(buffer...  18.5 us
    all_to_all x1, starting transfers between devices, row_exchange(): lax.all_to_all(slab.reshape(rows, n, order // n), 'row', split_axis=1, co...  4.53 us
    pallas_call x2, Pallas kernels, prepare(): pl.pallas_call(prepare_kernel, out_shape=[jax.ShapeDtypeStruct((k, m), jn...  3.68 us
  transfers between devices with their start and end apart: 37, of which 18 were waited for; matrix products, arithmetic and copies ran while one was open for 1% of the time, Pallas kernels for 11%

profile of v3, /device:TPU:24, one launch (start us, length us, event | category | flops | bytes accessed | tf_op | source)
XLA Modules:
  0.0 169.8 jit_solution(13037738361319792767)
XLA Ops:
  0.0 1.1 constant_dynamic-slice_fusion.3
  1.1 3.1 %collective-permute-start.12 = (f32[4,8,1024]{2,1,0:T(8,128)S(1)}, f32[4,8,1024]{2,1,0:T(8,128)S(1)}, u32[]{:S(2)}, u32[]{:S(2)}) collective-permute-start(f32[4,8,1024]{2,1,0:T(8,128)S(1)} %bitcast.38), channel_id=1, source_target_pairs={{8,0},{9,1},{10,2},{11,3},{12,4},{13,5},{14,6},{15,7},{0,8},{1,9},... | collective-permute-start | bytes 393224 | tf_op jit(solution)/shard_map/ppermute | solution.py:39
  4.2 0.6 collective-permute-start.11
  4.8 2.6 %collective-permute-start.10 = (f32[4,8,1024]{2,1,0:T(8,128)S(1)}, f32[4,8,1024]{2,1,0:T(8,128)S(1)}, u32[]{:S(2)}, u32[]{:S(2)}) collective-permute-start(f32[4,8,1024]{2,1,0:T(8,128)S(1)} %bitcast.35), channel_id=1, source_target_pairs={{4,0},{5,1},{6,2},{7,3},{8,4},{9,5},{10,6},{11,7},{12,8},{13,9},{1... | collective-permute-start | bytes 393224 | tf_op jit(solution)/shard_map/ppermute | solution.py:39
  7.5 1.5 collective-permute-done.12
  9.0 2.1 %collective-permute-done.11 = f32[4,8,1024]{2,1,0:T(8,128)S(1)} collective-permute-done((f32[4,8,1024]{2,1,0:T(8,128)S(1)}, f32[4,8,1024]{2,1,0:T(8,128)S(1)}, u32[]{:S(2)}, u32[]{:S(2)}) %collective-permute-start.11) | collective-permute-done | bytes 131104 | tf_op jit(solution)/shard_map/ppermute | solution.py:39
  11.2 7.3 %collective-permute-start.15 = (f32[4,8,1024]{2,1,0:T(8,128)S(1)}, f32[4,8,1024]{2,1,0:T(8,128)S(1)}, u32[]{:S(2)}, u32[]{:S(2)}) collective-permute-start(f32[4,8,1024]{2,1,0:T(8,128)S(1)} %get-tuple-element.30), channel_id=1, source_target_pairs={{2,0},{3,1},{0,2},{1,3},{6,4},{7,5},{4,6},{5,7},{10,8},{11,9},{8,1... | collective-permute-start | bytes 393224 | tf_op jit(solution)/shard_map/ppermute | solution.py:39
  18.5 1.5 collective-permute-start.14
  19.9 2.7 %collective-permute-start.13 = (f32[4,8,1024]{2,1,0:T(8,128)S(1)}, f32[4,8,1024]{2,1,0:T(8,128)S(1)}, u32[]{:S(2)}, u32[]{:S(2)}) collective-permute-start(f32[4,8,1024]{2,1,0:T(8,128)S(1)} %get-tuple-element.32), channel_id=1, source_target_pairs={{1,0},{2,1},{3,2},{0,3},{5,4},{6,5},{7,6},{4,7},{9,8},{10,9},{11,1... | collective-permute-start | bytes 393224 | tf_op jit(solution)/shard_map/ppermute | solution.py:39
  22.6 2.3 %collective-permute-done.15 = f32[4,8,1024]{2,1,0:T(8,128)S(1)} collective-permute-done((f32[4,8,1024]{2,1,0:T(8,128)S(1)}, f32[4,8,1024]{2,1,0:T(8,128)S(1)}, u32[]{:S(2)}, u32[]{:S(2)}) %collective-permute-start.15) | collective-permute-done | bytes 131104 | tf_op jit(solution)/shard_map/ppermute | solution.py:39
  24.9 3.7 %collective-permute-done.14 = f32[4,8,1024]{2,1,0:T(8,128)S(1)} collective-permute-done((f32[4,8,1024]{2,1,0:T(8,128)S(1)}, f32[4,8,1024]{2,1,0:T(8,128)S(1)}, u32[]{:S(2)}, u32[]{:S(2)}) %collective-permute-start.14) | collective-permute-done | bytes 131104 | tf_op jit(solution)/shard_map/ppermute | solution.py:39
  28.6 1.9 %collective-permute-done.13 = f32[4,8,1024]{2,1,0:T(8,128)S(1)} collective-permute-done((f32[4,8,1024]{2,1,0:T(8,128)S(1)}, f32[4,8,1024]{2,1,0:T(8,128)S(1)}, u32[]{:S(2)}, u32[]{:S(2)}) %collective-permute-start.13) | collective-permute-done | bytes 131104 | tf_op jit(solution)/shard_map/ppermute | solution.py:39
  30.6 0.8 collective-permute-start.17
  31.4 2.5 %collective-permute-start.19 = (f32[16,8,1024]{2,1,0:T(8,128)S(1)}, f32[16,8,1024]{2,1,0:T(8,128)S(1)}, u32[]{:S(2)}, u32[]{:S(2)}) collective-permute-start(f32[16,8,1024]{2,1,0:T(8,128)S(1)} %pad_maximum_fusion.1.refs_0_), channel_id=1, source_target_pairs={{192,0},{193,1},{194,2},{195,3},{196,4},{197,5},{198,6},{199,7},{2... | collective-permute-start | bytes 1572872 | tf_op jit(solution)/shard_map/ppermute | solution.py:39
  33.9 4.5 %all-to-all-start = ((f32[8,16,1024]{2,0,1:T(8,128)}), f32[8,16,1024]{2,0,1:T(8,128)S(1)}, u32[]{:S(2)}, u32[]{:S(2)}) async-start(f32[8,16,1024]{2,0,1:T(8,128)} %bitcast.1), calls=%async_computation | async-start | bytes 1048576 | tf_op jit(solution)/shard_map/all_to_all | solution.py:50
  38.4 1.5 collective-permute-start.27
  39.9 0.0 collective-permute-start.16
  39.9 10.7 %collective-permute-done.17.refs_2_ = f32[16,8,1024]{2,1,0:T(8,128)S(1)} collective-permute-done((f32[16,8,1024]{2,1,0:T(8,128)S(1)}, f32[16,8,1024]{2,1,0:T(8,128)S(1)}, u32[]{:S(2)}, u32[]{:S(2)}) %collective-permute-start.17) | collective-permute-done | bytes 524320 | tf_op jit(solution)/shard_map/ppermute | solution.py:39
  50.6 0.5 collective-permute-start.20
  51.1 0.9 broadcast_select_fusion.2
  51.9 6.1 %collective-permute-done.27.refs_0_ = f32[16,8,1024]{2,1,0:T(8,128)} collective-permute-done((f32[16,8,1024]{2,1,0:T(8,128)S(1)}, f32[16,8,1024]{2,1,0:T(8,128)}, u32[]{:S(2)}, u32[]{:S(2)}) %collective-permute-start.27) | collective-permute-done | bytes 524320 | tf_op jit(solution)/shard_map/ppermute | solution.py:39
  58.0 0.0 collective-permute-start.28
  58.0 0.0 collective-permute-done.16.refs_1_
  58.0 0.8 copy-done.1
  58.8 0.9 collective-permute-start.29
  59.7 0.8 copy-done.3
  60.5 2.4 %collective-permute-start.31 = (f32[16,8,1024]{2,1,0:T(8,128)}, f32[16,8,1024]{2,1,0:T(8,128)S(1)}, u32[]{:S(2)}, u32[]{:S(2)}) collective-permute-start(f32[16,8,1024]{2,1,0:T(8,128)} %collective-permute-done.27.refs_0_), channel_id=1, source_target_pairs={{192,0},{193,1},{194,2},{195,3},{196,4},{197,5},{198,6},{199,7},{2... | collective-permute-start | bytes 1572872 | tf_op jit(solution)/shard_map/ppermute | solution.py:39
  62.9 0.0 copy-start
  62.9 2.6 %collective-permute-start = (f32[16,8,1024]{2,1,0:T(8,128)S(1)}, f32[16,8,1024]{2,1,0:T(8,128)S(1)}, u32[]{:S(2)}, u32[]{:S(2)}) collective-permute-start(f32[16,8,1024]{2,1,0:T(8,128)S(1)} %bitcast.28), channel_id=1, source_target_pairs={{4,0},{5,1},{6,2},{7,3},{8,4},{9,5},{10,6},{11,7},{12,8},{13,9},{1... | collective-permute-start | bytes 1572872 | tf_op jit(solution)/shard_map/ppermute | solution.py:39
  65.5 0.0 collective-permute-start.1
  65.5 4.1 %collective-permute-start.3 = (f32[16,8,1024]{2,1,0:T(8,128)S(1)}, f32[16,8,1024]{2,1,0:T(8,128)S(1)}, u32[]{:S(2)}, u32[]{:S(2)}) collective-permute-start(f32[16,8,1024]{2,1,0:T(8,128)S(1)} %bitcast.30), channel_id=1, source_target_pairs={{1,0},{2,1},{3,2},{0,3},{5,4},{6,5},{7,6},{4,7},{9,8},{10,9},{11,1... | collective-permute-start | bytes 1572872 | tf_op jit(solution)/shard_map/ppermute | solution.py:39
  69.7 4.9 %collective-permute-done.29.refs_2_ = f32[16,8,1024]{2,1,0:T(8,128)S(1)} collective-permute-done((f32[16,8,1024]{2,1,0:T(8,128)}, f32[16,8,1024]{2,1,0:T(8,128)S(1)}, u32[]{:S(2)}, u32[]{:S(2)}) %collective-permute-start.29) | collective-permute-done | bytes 524320 | tf_op jit(solution)/shard_map/ppermute | solution.py:39
  74.6 2.1 %collective-permute-start.4 = (f32[16,8,1024]{2,1,0:T(8,128)S(1)}, f32[16,8,1024]{2,1,0:T(8,128)S(1)}, u32[]{:S(2)}, u32[]{:S(2)}) collective-permute-start(f32[16,8,1024]{2,1,0:T(8,128)S(1)} %bitcast.31), channel_id=1, source_target_pairs={{3,0},{0,1},{1,2},{2,3},{7,4},{4,5},{5,6},{6,7},{11,8},{8,9},{9,10... | collective-permute-start | bytes 1572872 | tf_op jit(solution)/shard_map/ppermute | solution.py:39
  76.7 0.1 broadcast_select_fusion.1
  76.7 0.1 collective-permute-done.refs_1_
  76.8 0.5 collective-permute-start.30
  77.3 2.9 %collective-permute-done.1.refs_2_ = f32[16,8,1024]{2,1,0:T(8,128)S(1)} collective-permute-done((f32[16,8,1024]{2,1,0:T(8,128)S(1)}, f32[16,8,1024]{2,1,0:T(8,128)S(1)}, u32[]{:S(2)}, u32[]{:S(2)}) %collective-permute-start.1) | collective-permute-done | bytes 524320 | tf_op jit(solution)/shard_map/ppermute | solution.py:39
  80.2 0.1 broadcast_select_fusion.4
  80.3 11.0 %collective-permute-done.3.refs_4_ = f32[16,8,1024]{2,1,0:T(8,128)S(1)} collective-permute-done((f32[16,8,1024]{2,1,0:T(8,128)S(1)}, f32[16,8,1024]{2,1,0:T(8,128)S(1)}, u32[]{:S(2)}, u32[]{:S(2)}) %collective-permute-start.3) | collective-permute-done | bytes 524320 | tf_op jit(solution)/shard_map/ppermute | solution.py:39
  91.3 10.2 %collective-permute-done.4.refs_5_ = f32[16,8,1024]{2,1,0:T(8,128)S(1)} collective-permute-done((f32[16,8,1024]{2,1,0:T(8,128)S(1)}, f32[16,8,1024]{2,1,0:T(8,128)S(1)}, u32[]{:S(2)}, u32[]{:S(2)}) %collective-permute-start.4) | collective-permute-done | bytes 524320 | tf_op jit(solution)/shard_map/ppermute | solution.py:39
  101.6 2.7 %collective-permute-start.2 = (f32[16,8,1024]{2,1,0:T(8,128)S(1)}, f32[16,8,1024]{2,1,0:T(8,128)S(1)}, u32[]{:S(2)}, u32[]{:S(2)}) collective-permute-start(f32[16,8,1024]{2,1,0:T(8,128)S(1)} %broadcast_select_fusion.4), channel_id=1, source_target_pairs={{4,0},{5,1},{6,2},{7,3},{8,4},{9,5},{10,6},{11,7},{12,8},{13,9},{1... | collective-permute-start | bytes 1572872 | tf_op jit(solution)/shard_map/ppermute | solution.py:39
  104.3 0.0 collective-permute-start.5
  104.3 0.1 broadcast_select_fusion.3
  104.4 2.6 %collective-permute-start.9 = (f32[16,8,1024]{2,1,0:T(8,128)S(1)}, f32[16,8,1024]{2,1,0:T(8,128)S(1)}, u32[]{:S(2)}, u32[]{:S(2)}) collective-permute-start(f32[16,8,1024]{2,1,0:T(8,128)S(1)} %broadcast_select_fusion.3), channel_id=1, source_target_pairs={{1,0},{2,1},{3,2},{0,3},{5,4},{6,5},{7,6},{4,7},{9,8},{10,9},{11,1... | collective-permute-start | bytes 1572872 | tf_op jit(solution)/shard_map/ppermute | solution.py:39
  107.0 2.0 %collective-permute-start.6 = (f32[16,8,1024]{2,1,0:T(8,128)S(1)}, f32[16,8,1024]{2,1,0:T(8,128)S(1)}, u32[]{:S(2)}, u32[]{:S(2)}) collective-permute-start(f32[16,8,1024]{2,1,0:T(8,128)S(1)} %collective-permute-done.3.refs_4_), channel_id=1, source_target_pairs={{12,0},{13,1},{14,2},{15,3},{0,4},{1,5},{2,6},{3,7},{4,8},{5,9},{6... | collective-permute-start | bytes 1572872 | tf_op jit(solution)/shard_map/ppermute | solution.py:39
  109.0 1.2 collective-permute-start.7
  110.3 6.3 %collective-permute-done.2.refs_3_ = f32[16,8,1024]{2,1,0:T(8,128)S(1)} collective-permute-done((f32[16,8,1024]{2,1,0:T(8,128)S(1)}, f32[16,8,1024]{2,1,0:T(8,128)S(1)}, u32[]{:S(2)}, u32[]{:S(2)}) %collective-permute-start.2) | collective-permute-done | bytes 524320 | tf_op jit(solution)/shard_map/ppermute | solution.py:39
  116.6 1.6 collective-permute-start.8
  118.2 9.0 %collective-permute-done.5.refs_6_ = f32[16,8,1024]{2,1,0:T(8,128)S(1)} collective-permute-done((f32[16,8,1024]{2,1,0:T(8,128)S(1)}, f32[16,8,1024]{2,1,0:T(8,128)S(1)}, u32[]{:S(2)}, u32[]{:S(2)}) %collective-permute-start.5) | collective-permute-done | bytes 524320 | tf_op jit(solution)/shard_map/ppermute | solution.py:39
  127.2 2.5 %collective-permute-start.25 = (f32[16,8,1024]{2,1,0:T(8,128)S(1)}, f32[16,8,1024]{2,1,0:T(8,128)S(1)}, u32[]{:S(2)}, u32[]{:S(2)}) collective-permute-start(f32[16,8,1024]{2,1,0:T(8,128)S(1)} %collective-permute-done.9.refs_10_), channel_id=1, source_target_pairs={{4,0},{5,1},{6,2},{7,3},{8,4},{9,5},{10,6},{11,7},{12,8},{13,9},{1... | collective-permute-start | bytes 1572872 | tf_op jit(solution)/shard_map/ppermute | solution.py:39
  129.7 1.8 %shard_map.28 = (bf16[704,1024]{1,0:T(8,128)(2,1)S(1)}, bf16[704,1024]{1,0:T(8,128)(2,1)S(1)}, bf16[256,1024]{1,0:T(8,128)(2,1)S(1)}, bf16[256,1024]{1,0:T(8,128...) custom-call(f32[16,8,1024]{2,1,0:T(8,128)S(1)} %pad_maximum_fusion.1.refs_0_, ...), custom_call_target="tpu_custom_call" | custom-call | flops 4194304 | bytes 8388608 | tf_op jit(solution)/shard_map/pallas_call | solution.py:97
  131.6 3.7 %collective-permute-done.7.refs_8_ = f32[16,8,1024]{2,1,0:T(8,128)S(1)} collective-permute-done((f32[16,8,1024]{2,1,0:T(8,128)S(1)}, f32[16,8,1024]{2,1,0:T(8,128)S(1)}, u32[]{:S(2)}, u32[]{:S(2)}) %collective-permute-start.7) | collective-permute-done | bytes 524320 | tf_op jit(solution)/shard_map/ppermute | solution.py:39
  135.3 1.3 collective-permute-start.23
  136.6 0.7 collective-permute-start.24
  137.4 5.8 %shard_map.29.acc = f32[1024,1024]{1,0:T(8,128)S(1)} custom-call(s32[1]{0:T(128)} %bitcast.place, f32[1024,1024]{1,0:T(8,128)S(1)} %copy-done, f32[16,8,1024]{2,1,0:T(8,128)S(1)} %bitcast.32, f32[16,8,1024]{2,1,0:T(8,128)S(1)} %collective-permute-done.refs_1_, f32[16,8,1024]{2,1,0:T(8,128)S(1)} %collective-permute-done.1.refs_2_, ...), custom_call_target="tpu_custom_call" | custom-call | flops 4429185024 | bytes 14155776 | tf_op jit(solution)/shard_map/pallas_call | solution.py:189
  143.2 1.8 %shard_map.31 = (bf16[704,1024]{1,0:T(8,128)(2,1)S(1)}, bf16[704,1024]{1,0:T(8,128)(2,1)S(1)}, bf16[256,1024]{1,0:T(8,128)(2,1)S(1)}, bf16[256,1024]{1,0:T(8,128...) custom-call(f32[16,8,1024]{2,1,0:T(8,128)} %collective-permute-done.27.refs_0_, ...), custom_call_target="tpu_custom_call" | custom-call | flops 4194304 | bytes 8388608 | tf_op jit(solution)/shard_map/pallas_call | solution.py:97
  145.0 1.5 collective-permute-done.25.refs_2_.refs_13_
  146.6 0.1 broadcast_select_fusion
  146.6 1.4 collective-permute-start.35
  148.0 7.3 %collective-permute-done.23.refs_0_.refs_11_ = f32[16,8,1024]{2,1,0:T(8,128)S(1)} collective-permute-done((f32[16,8,1024]{2,1,0:T(8,128)S(1)}, f32[16,8,1024]{2,1,0:T(8,128)S(1)}, u32[]{:S(2)}, u32[]{:S(2)}) %collective-permute-start.23) | collective-permute-done | bytes 524320 | tf_op jit(solution)/shard_map/ppermute | solution.py:39
  155.3 1.7 collective-permute-done.24.refs_1_.refs_12_
  157.0 2.2 %shard_map.30.acc = f32[1024,1024]{1,0:T(8,128)S(1)} custom-call(s32[1]{0:T(128)} %bitcast.place, f32[1024,1024]{1,0:T(8,128)S(1)} %shard_map.29.acc, f32[16,8,1024]{2,1,0:T(8,128)S(1)} %collective-permute-done.23.refs_0_.refs_11_, f32[16,8,1024]{2,1,0:T(8,128)S(1)} %collective-permute-done.24.refs_1_.refs_12_, ...), custom_call_target="tpu_custom_call" | custom-call | flops 1610612736 | bytes 10485760 | tf_op jit(solution)/shard_map/pallas_call | solution.py:189
  159.2 7.6 %shard_map.32.acc = f32[1024,1024]{1,0:T(8,128)S(1)} custom-call(s32[1]{0:T(128)} %bitcast.place, f32[1024,1024]{1,0:T(8,128)S(1)} %shard_map.30.acc, f32[16,8,1024]{2,1,0:T(8,128)S(1)} %bitcast.33, f32[16,8,1024]{2,1,0:T(8,128)S(1)} %collective-permute-done.refs_1_, f32[16,8,1024]{2,1,0:T(8,128)S(1)} %collective-permute-done.1.refs_2_, ...), custom_call_target="tpu_custom_call" | custom-call | flops 6039797760 | bytes 16252928 | tf_op jit(solution)/shard_map/pallas_call | solution.py:189
  166.8 2.8 %shard_map.33 = f32[1024,1024]{1,0:T(8,128)} custom-call(s32[1]{0:T(128)} %bitcast.place, f32[1024,1024]{1,0:T(8,128)S(1)} %shard_map.32.acc, f32[16,8,1024]{2,1,0:T(8,128)S(1)} %collective-permute-done.35.refs_0_, bf16[64,1024]{1,0:T(8,128)(2,1)S(1)} %get-tuple-element.25.refs_1_, bf16[64,1024]{1,0:T(8,128)(2,1)S(1)} %get-tuple-element.26.refs_2_, ...), custom_call_target="tpu_custom_call" | custom-call | flops 805306368 | bytes 9437184 | tf_op jit(solution)/shard_map/pallas_call | solution.py:189
  (35 shorter events, 0.2 us)
Async XLA Ops:
  1.1 7.8 %collective-permute-start.12 = (f32[4,8,1024]{2,1,0:T(8,128)S(1)}, f32[4,8,1024]{2,1,0:T(8,128)S(1)}, u32[]{:S(2)}, u32[]{:S(2)}) collective-permute-start(f32[4,8,1024]{2,1,0:T(8,128)S(1)} %bitcast.38), channel_id=1, source_target_pairs={{8,0},{9,1},{10,2},{11,3},{12,4},{13,5},{14,6},{15,7},{0,8},{1,9},... | collective-permute-start | bytes 393224 | tf_op jit(solution)/shard_map/ppermute | solution.py:39
  4.2 6.8 %collective-permute-start.11 = (f32[4,8,1024]{2,1,0:T(8,128)S(1)}, f32[4,8,1024]{2,1,0:T(8,128)S(1)}, u32[]{:S(2)}, u32[]{:S(2)}) collective-permute-start(f32[4,8,1024]{2,1,0:T(8,128)S(1)} %bitcast.36), channel_id=1, source_target_pairs={{12,0},{13,1},{14,2},{15,3},{0,4},{1,5},{2,6},{3,7},{4,8},{5,9},{6... | collective-permute-start | bytes 393224 | tf_op jit(solution)/shard_map/ppermute | solution.py:39
  4.8 6.3 %collective-permute-start.10 = (f32[4,8,1024]{2,1,0:T(8,128)S(1)}, f32[4,8,1024]{2,1,0:T(8,128)S(1)}, u32[]{:S(2)}, u32[]{:S(2)}) collective-permute-start(f32[4,8,1024]{2,1,0:T(8,128)S(1)} %bitcast.35), channel_id=1, source_target_pairs={{4,0},{5,1},{6,2},{7,3},{8,4},{9,5},{10,6},{11,7},{12,8},{13,9},{1... | collective-permute-start | bytes 393224 | tf_op jit(solution)/shard_map/ppermute | solution.py:39
  11.2 13.7 %collective-permute-start.15 = (f32[4,8,1024]{2,1,0:T(8,128)S(1)}, f32[4,8,1024]{2,1,0:T(8,128)S(1)}, u32[]{:S(2)}, u32[]{:S(2)}) collective-permute-start(f32[4,8,1024]{2,1,0:T(8,128)S(1)} %get-tuple-element.30), channel_id=1, source_target_pairs={{2,0},{3,1},{0,2},{1,3},{6,4},{7,5},{4,6},{5,7},{10,8},{11,9},{8,1... | collective-permute-start | bytes 393224 | tf_op jit(solution)/shard_map/ppermute | solution.py:39
  18.5 10.2 %collective-permute-start.14 = (f32[4,8,1024]{2,1,0:T(8,128)S(1)}, f32[4,8,1024]{2,1,0:T(8,128)S(1)}, u32[]{:S(2)}, u32[]{:S(2)}) collective-permute-start(f32[4,8,1024]{2,1,0:T(8,128)S(1)} %get-tuple-element.31), channel_id=1, source_target_pairs={{3,0},{0,1},{1,2},{2,3},{7,4},{4,5},{5,6},{6,7},{11,8},{8,9},{9,10... | collective-permute-start | bytes 393224 | tf_op jit(solution)/shard_map/ppermute | solution.py:39
  19.9 10.6 %collective-permute-start.13 = (f32[4,8,1024]{2,1,0:T(8,128)S(1)}, f32[4,8,1024]{2,1,0:T(8,128)S(1)}, u32[]{:S(2)}, u32[]{:S(2)}) collective-permute-start(f32[4,8,1024]{2,1,0:T(8,128)S(1)} %get-tuple-element.32), channel_id=1, source_target_pairs={{1,0},{2,1},{3,2},{0,3},{5,4},{6,5},{7,6},{4,7},{9,8},{10,9},{11,1... | collective-permute-start | bytes 393224 | tf_op jit(solution)/shard_map/ppermute | solution.py:39
  30.6 20.0 %collective-permute-start.17 = (f32[16,8,1024]{2,1,0:T(8,128)S(1)}, f32[16,8,1024]{2,1,0:T(8,128)S(1)}, u32[]{:S(2)}, u32[]{:S(2)}) collective-permute-start(f32[16,8,1024]{2,1,0:T(8,128)S(1)} %pad_maximum_fusion.1.refs_0_), channel_id=1, source_target_pairs={{64,0},{65,1},{66,2},{67,3},{68,4},{69,5},{70,6},{71,7},{72,8},{73... | collective-permute-start | bytes 1572872 | tf_op jit(solution)/shard_map/ppermute | solution.py:39
  31.4 19.2 %collective-permute-start.19 = (f32[16,8,1024]{2,1,0:T(8,128)S(1)}, f32[16,8,1024]{2,1,0:T(8,128)S(1)}, u32[]{:S(2)}, u32[]{:S(2)}) collective-permute-start(f32[16,8,1024]{2,1,0:T(8,128)S(1)} %pad_maximum_fusion.1.refs_0_), channel_id=1, source_target_pairs={{192,0},{193,1},{194,2},{195,3},{196,4},{197,5},{198,6},{199,7},{2... | collective-permute-start | bytes 1572872 | tf_op jit(solution)/shard_map/ppermute | solution.py:39
  33.9 29.0 %all-to-all-start = ((f32[8,16,1024]{2,0,1:T(8,128)}), f32[8,16,1024]{2,0,1:T(8,128)S(1)}, u32[]{:S(2)}, u32[]{:S(2)}) async-start(f32[8,16,1024]{2,0,1:T(8,128)} %bitcast.1), calls=%async_computation | async-start | bytes 1048576 | tf_op jit(solution)/shard_map/all_to_all | solution.py:50
  38.4 19.6 %collective-permute-start.27 = (f32[16,8,1024]{2,1,0:T(8,128)S(1)}, f32[16,8,1024]{2,1,0:T(8,128)}, u32[]{:S(2)}, u32[]{:S(2)}) collective-permute-start(f32[16,8,1024]{2,1,0:T(8,128)S(1)} %pad_maximum_fusion.1.refs_0_), channel_id=1, source_target_pairs={{32,0},{33,1},{34,2},{35,3},{36,4},{37,5},{38,6},{39,7},{40,8},{41... | collective-permute-start | bytes 1572872 | tf_op jit(solution)/shard_map/ppermute | solution.py:39
  39.9 18.1 %collective-permute-start.16 = (f32[16,8,1024]{2,1,0:T(8,128)S(1)}, f32[16,8,1024]{2,1,0:T(8,128)S(1)}, u32[]{:S(2)}, u32[]{:S(2)}) collective-permute-start(f32[16,8,1024]{2,1,0:T(8,128)S(1)} %pad_maximum_fusion.1.refs_0_), channel_id=1, source_target_pairs={{16,0},{17,1},{18,2},{19,3},{20,4},{21,5},{22,6},{23,7},{24,8},{25... | collective-permute-start | bytes 1572872 | tf_op jit(solution)/shard_map/ppermute | solution.py:39
  50.6 9.1 %collective-permute-start.18 = (f32[16,8,1024]{2,1,0:T(8,128)S(1)}, f32[16,8,1024]{2,1,0:T(8,128)S(1)}, u32[]{:S(2)}, u32[]{:S(2)}) collective-permute-start(f32[16,8,1024]{2,1,0:T(8,128)S(1)} %collective-permute-done.17.refs_2_), channel_id=1, source_target_pairs={{16,0},{17,1},{18,2},{19,3},{20,4},{21,5},{22,6},{23,7},{24,8},{25... | collective-permute-start | bytes 1572872 | tf_op jit(solution)/shard_map/ppermute | solution.py:39
  50.6 12.3 %collective-permute-start.20 = (f32[16,8,1024]{2,1,0:T(8,128)S(1)}, f32[16,8,1024]{2,1,0:T(8,128)}, u32[]{:S(2)}, u32[]{:S(2)}) collective-permute-start(f32[16,8,1024]{2,1,0:T(8,128)S(1)} %collective-permute-done.19.refs_4_), channel_id=1, source_target_pairs={{16,0},{17,1},{18,2},{19,3},{20,4},{21,5},{22,6},{23,7},{24,8},{25... | collective-permute-start | bytes 1572872 | tf_op jit(solution)/shard_map/ppermute | solution.py:39
  51.9 13.6 %collective-permute-start.21 = (f32[16,8,1024]{2,1,0:T(8,128)}, f32[16,8,1024]{2,1,0:T(8,128)}, u32[]{:S(2)}, u32[]{:S(2)}) collective-permute-start(f32[16,8,1024]{2,1,0:T(8,128)} %broadcast_select_fusion.2), channel_id=1, source_target_pairs={{64,0},{65,1},{66,2},{67,3},{68,4},{69,5},{70,6},{71,7},{72,8},{73... | collective-permute-start | bytes 1572872 | tf_op jit(solution)/shard_map/ppermute | solution.py:39
  58.0 7.5 %collective-permute-start.28 = (f32[16,8,1024]{2,1,0:T(8,128)}, f32[16,8,1024]{2,1,0:T(8,128)}, u32[]{:S(2)}, u32[]{:S(2)}) collective-permute-start(f32[16,8,1024]{2,1,0:T(8,128)} %collective-permute-done.27.refs_0_), channel_id=1, source_target_pairs={{16,0},{17,1},{18,2},{19,3},{20,4},{21,5},{22,6},{23,7},{24,8},{25... | collective-permute-start | bytes 1572872 | tf_op jit(solution)/shard_map/ppermute | solution.py:39
  58.0 0.8 copy-start.1
  58.8 15.8 %collective-permute-start.29 = (f32[16,8,1024]{2,1,0:T(8,128)}, f32[16,8,1024]{2,1,0:T(8,128)S(1)}, u32[]{:S(2)}, u32[]{:S(2)}) collective-permute-start(f32[16,8,1024]{2,1,0:T(8,128)} %collective-permute-done.27.refs_0_), channel_id=1, source_target_pairs={{64,0},{65,1},{66,2},{67,3},{68,4},{69,5},{70,6},{71,7},{72,8},{73... | collective-permute-start | bytes 1572872 | tf_op jit(solution)/shard_map/ppermute | solution.py:39
  59.7 0.8 copy-start.3
  60.5 16.2 %collective-permute-start.31 = (f32[16,8,1024]{2,1,0:T(8,128)}, f32[16,8,1024]{2,1,0:T(8,128)S(1)}, u32[]{:S(2)}, u32[]{:S(2)}) collective-permute-start(f32[16,8,1024]{2,1,0:T(8,128)} %collective-permute-done.27.refs_0_), channel_id=1, source_target_pairs={{192,0},{193,1},{194,2},{195,3},{196,4},{197,5},{198,6},{199,7},{2... | collective-permute-start | bytes 1572872 | tf_op jit(solution)/shard_map/ppermute | solution.py:39
  62.9 66.9 %copy-start.2 = (f32[16,8,1024]{2,1,0:T(8,128)S(1)}, f32[16,8,1024]{2,1,0:T(8,128)}, u32[]{:S(2)}) copy-start(f32[16,8,1024]{2,1,0:T(8,128)} %copy-done.1) | copy-start | bytes 1572868
  62.9 66.9 %copy-start.4 = (f32[16,8,1024]{2,1,0:T(8,128)S(1)}, f32[16,8,1024]{2,1,0:T(8,128)}, u32[]{:S(2)}) copy-start(f32[16,8,1024]{2,1,0:T(8,128)} %copy-done.3) | copy-start | bytes 1572868
  62.9 74.5 %copy-start = (f32[1024,1024]{1,0:T(8,128)S(1)}, f32[1024,1024]{1,0:T(8,128)}, u32[]{:S(2)}) copy-start(f32[1024,1024]{1,0:T(8,128)} %acc.1) | copy-start | bytes 12582916
  62.9 13.9 %collective-permute-start = (f32[16,8,1024]{2,1,0:T(8,128)S(1)}, f32[16,8,1024]{2,1,0:T(8,128)S(1)}, u32[]{:S(2)}, u32[]{:S(2)}) collective-permute-start(f32[16,8,1024]{2,1,0:T(8,128)S(1)} %bitcast.28), channel_id=1, source_target_pairs={{4,0},{5,1},{6,2},{7,3},{8,4},{9,5},{10,6},{11,7},{12,8},{13,9},{1... | collective-permute-start | bytes 1572872 | tf_op jit(solution)/shard_map/ppermute | solution.py:39
  65.5 14.7 %collective-permute-start.1 = (f32[16,8,1024]{2,1,0:T(8,128)S(1)}, f32[16,8,1024]{2,1,0:T(8,128)S(1)}, u32[]{:S(2)}, u32[]{:S(2)}) collective-permute-start(f32[16,8,1024]{2,1,0:T(8,128)S(1)} %bitcast.29), channel_id=1, source_target_pairs={{12,0},{13,1},{14,2},{15,3},{0,4},{1,5},{2,6},{3,7},{4,8},{5,9},{6... | collective-permute-start | bytes 1572872 | tf_op jit(solution)/shard_map/ppermute | solution.py:39
  65.5 25.8 %collective-permute-start.3 = (f32[16,8,1024]{2,1,0:T(8,128)S(1)}, f32[16,8,1024]{2,1,0:T(8,128)S(1)}, u32[]{:S(2)}, u32[]{:S(2)}) collective-permute-start(f32[16,8,1024]{2,1,0:T(8,128)S(1)} %bitcast.30), channel_id=1, source_target_pairs={{1,0},{2,1},{3,2},{0,3},{5,4},{6,5},{7,6},{4,7},{9,8},{10,9},{11,1... | collective-permute-start | bytes 1572872 | tf_op jit(solution)/shard_map/ppermute | solution.py:39
  74.6 27.0 %collective-permute-start.4 = (f32[16,8,1024]{2,1,0:T(8,128)S(1)}, f32[16,8,1024]{2,1,0:T(8,128)S(1)}, u32[]{:S(2)}, u32[]{:S(2)}) collective-permute-start(f32[16,8,1024]{2,1,0:T(8,128)S(1)} %bitcast.31), channel_id=1, source_target_pairs={{3,0},{0,1},{1,2},{2,3},{7,4},{4,5},{5,6},{6,7},{11,8},{8,9},{9,10... | collective-permute-start | bytes 1572872 | tf_op jit(solution)/shard_map/ppermute | solution.py:39
  76.7 27.6 %collective-permute-start.22 = (f32[16,8,1024]{2,1,0:T(8,128)}, f32[16,8,1024]{2,1,0:T(8,128)S(1)}, u32[]{:S(2)}, u32[]{:S(2)}) collective-permute-start(f32[16,8,1024]{2,1,0:T(8,128)} %collective-permute-done.21.refs_6_), channel_id=1, source_target_pairs={{16,0},{17,1},{18,2},{19,3},{20,4},{21,5},{22,6},{23,7},{24,8},{25... | collective-permute-start | bytes 1572872 | tf_op jit(solution)/shard_map/ppermute | solution.py:39
  76.8 27.6 %collective-permute-start.30 = (f32[16,8,1024]{2,1,0:T(8,128)S(1)}, f32[16,8,1024]{2,1,0:T(8,128)S(1)}, u32[]{:S(2)}, u32[]{:S(2)}) collective-permute-start(f32[16,8,1024]{2,1,0:T(8,128)S(1)} %collective-permute-done.29.refs_2_), channel_id=1, source_target_pairs={{16,0},{17,1},{18,2},{19,3},{20,4},{21,5},{22,6},{23,7},{24,8},{25... | collective-permute-start | bytes 1572872 | tf_op jit(solution)/shard_map/ppermute | solution.py:39
  80.2 26.8 %collective-permute-start.32 = (f32[16,8,1024]{2,1,0:T(8,128)S(1)}, f32[16,8,1024]{2,1,0:T(8,128)S(1)}, u32[]{:S(2)}, u32[]{:S(2)}) collective-permute-start(f32[16,8,1024]{2,1,0:T(8,128)S(1)} %collective-permute-done.31.refs_4_), channel_id=1, source_target_pairs={{16,0},{17,1},{18,2},{19,3},{20,4},{21,5},{22,6},{23,7},{24,8},{25... | collective-permute-start | bytes 1572872 | tf_op jit(solution)/shard_map/ppermute | solution.py:39
  91.3 17.7 %collective-permute-start.33 = (f32[16,8,1024]{2,1,0:T(8,128)S(1)}, f32[16,8,1024]{2,1,0:T(8,128)S(1)}, u32[]{:S(2)}, u32[]{:S(2)}) collective-permute-start(f32[16,8,1024]{2,1,0:T(8,128)S(1)} %broadcast_select_fusion.1), channel_id=1, source_target_pairs={{64,0},{65,1},{66,2},{67,3},{68,4},{69,5},{70,6},{71,7},{72,8},{73... | collective-permute-start | bytes 1572872 | tf_op jit(solution)/shard_map/ppermute | solution.py:39
  101.6 15.0 %collective-permute-start.2 = (f32[16,8,1024]{2,1,0:T(8,128)S(1)}, f32[16,8,1024]{2,1,0:T(8,128)S(1)}, u32[]{:S(2)}, u32[]{:S(2)}) collective-permute-start(f32[16,8,1024]{2,1,0:T(8,128)S(1)} %broadcast_select_fusion.4), channel_id=1, source_target_pairs={{4,0},{5,1},{6,2},{7,3},{8,4},{9,5},{10,6},{11,7},{12,8},{13,9},{1... | collective-permute-start | bytes 1572872 | tf_op jit(solution)/shard_map/ppermute | solution.py:39
  104.3 22.9 %collective-permute-start.5 = (f32[16,8,1024]{2,1,0:T(8,128)S(1)}, f32[16,8,1024]{2,1,0:T(8,128)S(1)}, u32[]{:S(2)}, u32[]{:S(2)}) collective-permute-start(f32[16,8,1024]{2,1,0:T(8,128)S(1)} %collective-permute-done.3.refs_4_), channel_id=1, source_target_pairs={{4,0},{5,1},{6,2},{7,3},{8,4},{9,5},{10,6},{11,7},{12,8},{13,9},{1... | collective-permute-start | bytes 1572872 | tf_op jit(solution)/shard_map/ppermute | solution.py:39
  104.4 22.8 %collective-permute-start.9 = (f32[16,8,1024]{2,1,0:T(8,128)S(1)}, f32[16,8,1024]{2,1,0:T(8,128)S(1)}, u32[]{:S(2)}, u32[]{:S(2)}) collective-permute-start(f32[16,8,1024]{2,1,0:T(8,128)S(1)} %broadcast_select_fusion.3), channel_id=1, source_target_pairs={{1,0},{2,1},{3,2},{0,3},{5,4},{6,5},{7,6},{4,7},{9,8},{10,9},{11,1... | collective-permute-start | bytes 1572872 | tf_op jit(solution)/shard_map/ppermute | solution.py:39
  107.0 22.7 %collective-permute-start.6 = (f32[16,8,1024]{2,1,0:T(8,128)S(1)}, f32[16,8,1024]{2,1,0:T(8,128)S(1)}, u32[]{:S(2)}, u32[]{:S(2)}) collective-permute-start(f32[16,8,1024]{2,1,0:T(8,128)S(1)} %collective-permute-done.3.refs_4_), channel_id=1, source_target_pairs={{12,0},{13,1},{14,2},{15,3},{0,4},{1,5},{2,6},{3,7},{4,8},{5,9},{6... | collective-permute-start | bytes 1572872 | tf_op jit(solution)/shard_map/ppermute | solution.py:39
  109.0 26.3 %collective-permute-start.7 = (f32[16,8,1024]{2,1,0:T(8,128)S(1)}, f32[16,8,1024]{2,1,0:T(8,128)S(1)}, u32[]{:S(2)}, u32[]{:S(2)}) collective-permute-start(f32[16,8,1024]{2,1,0:T(8,128)S(1)} %collective-permute-done.4.refs_5_), channel_id=1, source_target_pairs={{4,0},{5,1},{6,2},{7,3},{8,4},{9,5},{10,6},{11,7},{12,8},{13,9},{1... | collective-permute-start | bytes 1572872 | tf_op jit(solution)/shard_map/ppermute | solution.py:39
  116.6 20.0 %collective-permute-start.8 = (f32[16,8,1024]{2,1,0:T(8,128)S(1)}, f32[16,8,1024]{2,1,0:T(8,128)S(1)}, u32[]{:S(2)}, u32[]{:S(2)}) collective-permute-start(f32[16,8,1024]{2,1,0:T(8,128)S(1)} %collective-permute-done.4.refs_5_), channel_id=1, source_target_pairs={{12,0},{13,1},{14,2},{15,3},{0,4},{1,5},{2,6},{3,7},{4,8},{5,9},{6... | collective-permute-start | bytes 1572872 | tf_op jit(solution)/shard_map/ppermute | solution.py:39
  127.2 16.0 %collective-permute-start.34 = (f32[16,8,1024]{2,1,0:T(8,128)S(1)}, f32[16,8,1024]{2,1,0:T(8,128)S(1)}, u32[]{:S(2)}, u32[]{:S(2)}) collective-permute-start(f32[16,8,1024]{2,1,0:T(8,128)S(1)} %collective-permute-done.33.refs_6_), channel_id=1, source_target_pairs={{16,0},{17,1},{18,2},{19,3},{20,4},{21,5},{22,6},{23,7},{24,8},{25... | collective-permute-start | bytes 1572872 | tf_op jit(solution)/shard_map/ppermute | solution.py:39
  127.2 19.4 %collective-permute-start.25 = (f32[16,8,1024]{2,1,0:T(8,128)S(1)}, f32[16,8,1024]{2,1,0:T(8,128)S(1)}, u32[]{:S(2)}, u32[]{:S(2)}) collective-permute-start(f32[16,8,1024]{2,1,0:T(8,128)S(1)} %collective-permute-done.9.refs_10_), channel_id=1, source_target_pairs={{4,0},{5,1},{6,2},{7,3},{8,4},{9,5},{10,6},{11,7},{12,8},{13,9},{1... | collective-permute-start | bytes 1572872 | tf_op jit(solution)/shard_map/ppermute | solution.py:39
  129.7 16.8 %collective-permute-start.26 = (f32[16,8,1024]{2,1,0:T(8,128)S(1)}, f32[16,8,1024]{2,1,0:T(8,128)S(1)}, u32[]{:S(2)}, u32[]{:S(2)}) collective-permute-start(f32[16,8,1024]{2,1,0:T(8,128)S(1)} %collective-permute-done.9.refs_10_), channel_id=1, source_target_pairs={{12,0},{13,1},{14,2},{15,3},{0,4},{1,5},{2,6},{3,7},{4,8},{5,9},{6... | collective-permute-start | bytes 1572872 | tf_op jit(solution)/shard_map/ppermute | solution.py:39
  135.3 20.0 %collective-permute-start.23 = (f32[16,8,1024]{2,1,0:T(8,128)S(1)}, f32[16,8,1024]{2,1,0:T(8,128)S(1)}, u32[]{:S(2)}, u32[]{:S(2)}) collective-permute-start(f32[16,8,1024]{2,1,0:T(8,128)S(1)} %collective-permute-done.5.refs_6_), channel_id=1, source_target_pairs={{4,0},{5,1},{6,2},{7,3},{8,4},{9,5},{10,6},{11,7},{12,8},{13,9},{1... | collective-permute-start | bytes 1572872 | tf_op jit(solution)/shard_map/ppermute | solution.py:39
  136.6 20.3 %collective-permute-start.24 = (f32[16,8,1024]{2,1,0:T(8,128)S(1)}, f32[16,8,1024]{2,1,0:T(8,128)S(1)}, u32[]{:S(2)}, u32[]{:S(2)}) collective-permute-start(f32[16,8,1024]{2,1,0:T(8,128)S(1)} %collective-permute-done.8.refs_9_), channel_id=1, source_target_pairs={{12,0},{13,1},{14,2},{15,3},{0,4},{1,5},{2,6},{3,7},{4,8},{5,9},{6... | collective-permute-start | bytes 1572872 | tf_op jit(solution)/shard_map/ppermute | solution.py:39
  146.6 20.2 %collective-permute-start.35 = (f32[16,8,1024]{2,1,0:T(8,128)S(1)}, f32[16,8,1024]{2,1,0:T(8,128)S(1)}, u32[]{:S(2)}, u32[]{:S(2)}) collective-permute-start(f32[16,8,1024]{2,1,0:T(8,128)S(1)} %broadcast_select_fusion), channel_id=1, source_target_pairs={{4,0},{5,1},{6,2},{7,3},{8,4},{9,5},{10,6},{11,7},{12,8},{13,9},{1... | collective-permute-start | bytes 1572872 | tf_op jit(solution)/shard_map/ppermute | solution.py:39
